TPU v7x, 32 devices: a whole 2x2x4 slice. The times are simulated.
32 devices in a mesh: group: 8 (over y, x, core), blk: 4 (over z).
Axes of the slice: x: 2, y: 2, z: 4, core: 2. Of those that a mesh axis runs over, the one named last changes fastest.
Arguments:
- front: float32 [8, 8192, 512], P('group', None, 'blk'), as said below
- child_blocks: float32 [8, 4, 8, 2, 128, 128], P('group', 'blk'), may hold values from -6 to 6
- child_rows: int32 [8, 4, 8, 2, 128], P('group', 'blk'), may hold values from 512 to 8191, as said below
- child_cols: int32 [8, 4, 8, 2, 128], P('group', 'blk'), may hold values from 0 to 127, each once within a row
- child_counts: int32 [8, 4, 8], P('group', 'blk'), may hold values from 0 to 2, as said below
Outputs:
- factors: float32 [8, 8192, 512], P('group', None, 'blk')
- pivots: float32 [8, 256], P('group')
Inputs may be any that keep to these rules, and one draw needn't show every extreme that they name: Rows 0 to 511 of each front form a symmetric matrix whose leading 2 * 128 rows and columns have a positive diagonal that dominates every row of that block; rows from 512 on are unstructured. `child_rows`: the 128 row indices of one slot are distinct and lie at or below row 512. `child_counts`: for every column block some destination group receives 2 live slots from every source group.
All inputs are finite; a program needn't handle non-finite values.
Results may differ from a plain program's by a relative error of at most 0.0003.
Values sent between devices are 32-bit elements; how exact they have to be, the bound alone decides.
No kernel may reach another device: no remote copies, remote signals or barrier semaphores. Data moves between devices by JAX's collectives and lax.ppermute only.
A program may use at most 64 MiB of HBM per device.

v0:
```python
import functools

import jax
import jax.numpy as jnp
from jax import lax
from jax.experimental import pallas as pl
from jax.experimental.pallas import tpu as pltpu
from jax.sharding import PartitionSpec as P


PANELS = 2
HIGHEST = lax.Precision.HIGHEST
VMEM = pl.BlockSpec(memory_space=pltpu.VMEM)
SMEM = pl.BlockSpec(memory_space=pltpu.SMEM)
ANY = pl.BlockSpec(memory_space=pl.ANY)
RAW_ROWS = 2048
FIRST_ROWS = 512
CHUNKS = 6


def dot(a, b, lhs=1, rhs=0):
    return lax.dot_general(
        a, b, (((lhs,), (rhs,)), ((), ())), precision=HIGHEST, preferred_element_type=jnp.float32
    )


def pack_kernel(counts_ref, partners_ref, blocks_ref, rows_ref, cols_ref, *refs):
    send_refs, (staged_ref, sem) = refs[:-2], refs[-2:]
    slots, width = rows_ref.shape[1], rows_ref.shape[2]
    target_ids = lax.broadcasted_iota(jnp.int32, (width, width), 0)
    copies = [
        pltpu.make_async_copy(blocks_ref.at[partners_ref[k]], staged_ref.at[k], sem.at[k])
        for k in range(len(send_refs))
    ]
    for copy in copies:
        copy.start()
    for k, send_ref in enumerate(send_refs):
        partner = partners_ref[k]
        copies[k].wait()
        live_slots = counts_ref[0, partner]
        indices = jnp.concatenate([rows_ref[partner], cols_ref[partner]], axis=0)
        for slot in range(slots):
            columns = jnp.broadcast_to(indices[slots + slot : slots + slot + 1, :], (width, width))
            placement = (columns == target_ids).astype(jnp.float32).astype(jnp.bfloat16)
            left = staged_ref[k, slot]
            placed = jnp.zeros((width, width), jnp.float32)
            for _ in range(3):
                term = left.astype(jnp.bfloat16)
                left = left - term.astype(jnp.float32)
                placed += lax.dot_general(
                    term, placement, (((1,), (1,)), ((), ())), preferred_element_type=jnp.float32
                )
            live = jnp.full((width, width), slot < live_slots)
            base = slot * (width + 8)
            send_ref[base : base + width, :] = jnp.where(live, placed, jnp.zeros_like(placed))
            row_ids = indices[slot : slot + 1, :].astype(jnp.float32)
            send_ref[base + width : base + width + 8, :] = jnp.broadcast_to(row_ids, (8, width))


def pack(blocks, rows, cols, counts, partners):
    groups, slots, width = rows.shape
    return pl.pallas_call(
        pack_kernel,
        in_specs=[SMEM, SMEM, ANY, VMEM, VMEM],
        out_specs=[VMEM] * groups,
        out_shape=[jax.ShapeDtypeStruct((slots * (width + 8), width), jnp.float32)] * groups,
        scratch_shapes=[
            pltpu.VMEM(blocks.shape, jnp.float32),
            pltpu.SemaphoreType.DMA((groups,)),
        ],
        name="pack",
    )(counts, partners, blocks, rows, cols)


def assemble_kernel(rows_ref, front_ref, *refs, window, sources, starts):
    block_refs, out_refs = refs[:sources], refs[sources:-4]
    sums_ref, staged_ref, front_sem, sem = refs[-4:]
    width = staged_ref.shape[2]
    height = width + 8
    slots = staged_ref.shape[1] // height
    rest = front_ref.shape[0] - window
    batch = 16
    loads = [pltpu.make_async_copy(front_ref.at[pl.ds(window, rest)], sums_ref, front_sem)]
    loads += [
        pltpu.make_async_copy(ref, staged_ref.at[i], sem.at[i]) for i, ref in enumerate(block_refs)
    ]
    for copy in loads:
        copy.start()
    for copy in loads:
        copy.wait()

    def add_block(block, carry):
        source, base = block // slots, lax.rem(block, slots) * height
        for first in range(0, width, batch):
            targets = [rows_ref[block, first + i] - window for i in range(batch)]
            sums = [
                sums_ref[pl.ds(targets[i], 1), :] + staged_ref[source, pl.ds(base + first + i, 1), :]
                for i in range(batch)
            ]
            for i in range(batch):
                sums_ref[pl.ds(targets[i], 1), :] = sums[i]
        return carry

    lax.fori_loop(0, sources * slots, add_block, 0)
    stores = [
        pltpu.make_async_copy(sums_ref.at[pl.ds(start - window, ref.shape[0])], ref, sem.at[i])
        for i, (start, ref) in enumerate(zip(starts, out_refs))
    ]
    for copy in stores:
        copy.start()
    for copy in stores:
        copy.wait()


def assemble(rows, blocks, front, window, starts, sizes):
    width = front.shape[1]
    return pl.pallas_call(
        functools.partial(assemble_kernel, window=window, sources=len(blocks), starts=starts),
        in_specs=[SMEM] + [ANY] * (1 + len(blocks)),
        out_specs=[ANY] * len(sizes),
        out_shape=[jax.ShapeDtypeStruct((size, width), jnp.float32) for size in sizes],
        scratch_shapes=[
            pltpu.VMEM((front.shape[0] - window, width), jnp.float32),
            pltpu.VMEM((len(blocks),) + blocks[0].shape, jnp.float32),
            pltpu.SemaphoreType.DMA,
            pltpu.SemaphoreType.DMA((max(len(blocks), len(sizes)),)),
        ],
        name="assemble",
    )(rows, front, *blocks)


def eliminate(m_ref, e_ref, wt_ref):
    size = m_ref.shape[0]
    row_ids = lax.broadcasted_iota(jnp.int32, (size, size), 0)
    col_ids = lax.broadcasted_iota(jnp.int32, (size, size), 1)
    e_ref[...] = (row_ids == col_ids).astype(jnp.float32)
    sub = lax.broadcasted_iota(jnp.int32, (8, size), 0)
    lane = lax.broadcasted_iota(jnp.int32, (1, size), 1)

    def step(k, diag):
        base = pl.multiple_of(k * 8, 8)
        rm, re = m_ref[pl.ds(base, 8), :], e_ref[pl.ds(base, 8), :]
        below = row_ids > base + 7
        m, e = m_ref[...], e_ref[...]
        scale = jnp.zeros((8, size), jnp.float32)
        for j in range(8):
            row_m, row_e = rm[j : j + 1, :], re[j : j + 1, :]
            pivot = rm[j : j + 1, j : j + 1]
            inverse = 1.0 / jnp.broadcast_to(pivot, (1, size))
            diag = jnp.where(lane == base + j, jnp.broadcast_to(pivot, (1, size)), diag)
            scale = jnp.where(sub == j, inverse, scale)
            l_r = jnp.where(sub > j, jnp.broadcast_to(rm[:, j : j + 1], (8, size)) * inverse, 0.0)
            rm, re = rm - l_r * row_m, re - l_r * row_e
            l_m = jnp.where(below, jnp.broadcast_to(m[:, j : j + 1], (size, size)) * inverse, 0.0)
            m, e = m - l_m * row_m, e - l_m * row_e
        m_ref[...] = pltpu.roll(m, size - 8, 1)
        e_ref[...] = e
        e_ref[pl.ds(base, 8), :] = re
        wt_ref[pl.ds(base, 8), :] = re * scale
        return diag

    return lax.fori_loop(0, size // 8, step, jnp.zeros((1, size), jnp.float32))


def factor_kernel(
    index_ref, tops_ref, own_ref, weights_ref, top_out_ref, pivots_ref, m_ref, e_ref, wt_ref, g_ref, h_ref
):
    blocks, width = tops_ref.shape[0], tops_ref.shape[2]
    mine = index_ref[0]

    def top(panel, block):
        place = lax.rem(mine - block + blocks, blocks)
        return tops_ref[place, panel * width : (panel + 1) * width, :]

    m_ref[...] = top(0, 0)
    pivots_ref[:, 0:width] = eliminate(m_ref, e_ref, wt_ref)
    wt_0, e_0 = wt_ref[...], e_ref[...]

    def panel_0(block, carry):
        rows = top(0, block)
        g_ref[0, block] = dot(wt_0, rows)
        h_ref[0, block] = dot(e_0, rows)
        return carry

    lax.fori_loop(0, blocks, panel_0, 0)
    g_01, h_01 = g_ref[0, 1], h_ref[0, 1]
    m_ref[...] = top(1, 1) - dot(g_01, h_01, 0, 0)
    pivots_ref[:, width:] = eliminate(m_ref, e_ref, wt_ref)
    wt_1, e_1 = wt_ref[...], e_ref[...]

    def panel_1(block, carry):
        rows = top(1, block) - dot(g_01, h_ref[0, block], 0, 0)
        g_ref[1, block] = dot(wt_1, rows)
        h_ref[1, block] = dot(e_1, rows)
        return carry

    g_ref[1, 0] = jnp.zeros_like(wt_1)
    lax.fori_loop(1, blocks, panel_1, 0)

    def update_weights(slot, block):
        y_1 = dot(wt_1, h_ref[1, block], 0, 0)
        weights_ref[slot, 0:width, :] = dot(wt_0, h_ref[0, block] - dot(h_01, y_1), 0, 0)
        weights_ref[slot, width:, :] = y_1

    for slot in range(1, weights_ref.shape[0]):
        update_weights(slot, slot + 1)

    @pl.when(mine == 0)
    def _():
        weights_ref[0, 0:width, :] = jnp.zeros_like(wt_0)
        weights_ref[0, width:, :] = wt_0.T

    @pl.when(mine == 1)
    def _():
        weights_ref[0, 0:width, :] = -dot(dot(wt_0, h_01, 0, 0), wt_1, 1, 1)
        weights_ref[0, width:, :] = wt_1.T

    @pl.when(mine > 1)
    def _():
        update_weights(0, mine)

    def top_rows(block, carry):
        rows = pl.ds(pl.multiple_of(block * width, width), width)

        @pl.when(mine <= 1)
        def _():
            top_out_ref[rows, :] = g_ref[mine, block].T

        @pl.when(mine > 1)
        def _():
            update = dot(g_ref[0, block], h_ref[0, mine], 0, 0)
            update += dot(g_ref[1, block], h_ref[1, mine], 0, 0)
            top_out_ref[rows, :] = own_ref[rows, :] - update

        return carry

    lax.fori_loop(0, blocks, top_rows, 0)


def factor(index, tops, own_top, slots):
    blocks, _, width = tops.shape
    window = blocks * width
    square = pltpu.VMEM((width, width), jnp.float32)
    panels = pltpu.VMEM((PANELS, blocks, width, width), jnp.float32)
    return pl.pallas_call(
        factor_kernel,
        in_specs=[SMEM, VMEM, VMEM],
        out_specs=[VMEM, VMEM, VMEM],
        out_shape=[
            jax.ShapeDtypeStruct((slots, 2 * width, width), jnp.float32),
            jax.ShapeDtypeStruct((window, width), jnp.float32),
            jax.ShapeDtypeStruct((1, 2 * width), jnp.float32),
        ],
        scratch_shapes=[square, square, square, panels, panels],
        name="factor",
    )(index, tops, own_top)


def multiply_kernel(left_ref, right_ref, weights_ref, *out_refs):
    width = left_ref.shape[1]
    for i, out_ref in enumerate(out_refs):
        out_ref[...] = dot(left_ref[...], weights_ref[i, 0:width, :]) + dot(
            right_ref[...], weights_ref[i, width:, :]
        )


def multiply(left, right, weights):
    rows, width = left.shape
    tile = 256
    spec = pl.BlockSpec((tile, width), lambda i: (i, 0))
    count = weights.shape[0]
    return pl.pallas_call(
        multiply_kernel,
        grid=(rows // tile,),
        in_specs=[spec, spec, pl.BlockSpec(weights.shape, lambda i: (0, 0, 0))],
        out_specs=[spec] * count,
        out_shape=[jax.ShapeDtypeStruct((rows, width), jnp.float32)] * count,
        name="multiply",
    )(left, right, weights)


def cut_rows(first, last):
    rest = last - first - RAW_ROWS - FIRST_ROWS
    size = -(-rest // ((CHUNKS - 1) * 256)) * 256
    sizes = [RAW_ROWS, FIRST_ROWS]
    while rest > 0:
        sizes.append(min(size, rest))
        rest -= sizes[-1]
    return [first + sum(sizes[:i]) for i in range(len(sizes))], sizes


def exchange(packed, groups):
    got = []
    for distance, block in packed:
        if distance == 0:
            got.append(block)
            continue
        pairs = [(i, i ^ distance) for i in range(groups)]
        got.append(lax.ppermute(block, "group", pairs))
    return got


def per_device(front, child_blocks, child_rows, child_cols, child_counts, *, blocks):
    return extend_and_factor(front[0], child_blocks[0, 0], child_rows[0, 0], child_cols[0, 0], child_counts[0], blocks)


def extend_and_factor(own, child_blocks, child_rows, child_cols, child_counts, blocks):
    total, width = own.shape
    window = blocks * width
    groups, slots = child_rows.shape[:2]
    mine = lax.axis_index("blk")
    index = mine.astype(jnp.int32).reshape(1)

    top = own[: 2 * width]
    tops = [top]
    for shift in range(1, blocks):
        pairs = [(i, (i + shift) % blocks) for i in range(blocks)]
        tops.append(lax.ppermute(top, "blk", pairs))

    distances = sorted(range(groups), key=lambda d: (-bin(d >> 1).count("1"), -d))
    partners = jnp.array(distances, jnp.int32) ^ lax.axis_index("group").astype(jnp.int32)
    packed = pack(child_blocks, child_rows, child_cols, child_counts, partners)
    got = exchange(list(zip(distances, packed)), groups)
    row_lines = [slot * (width + 8) + width for slot in range(slots)]
    rows = jnp.concatenate([g[i : i + 1] for g in got for i in row_lines]).astype(jnp.int32)
    starts, sizes = cut_rows(window, total)
    chunks = assemble(rows, got, own, window, starts, sizes)

    def finish(out, start, own_rows, first, update):
        mixed = jnp.where(mine <= 1, first, own_rows - update)
        return lax.dynamic_update_slice(out, mixed, (start, 0))

    if blocks > 4:
        weights, top_out, pivots = factor(index, jnp.stack(tops), own[:window], 1)
        out = lax.dynamic_update_slice(jnp.zeros_like(own), top_out, (0, 0))
        for start, chunk in zip(starts, chunks):
            out, chunk = lax.optimization_barrier((out, chunk))
            left, right = (
                lax.psum(jnp.where(mine == owner, chunk, 0.0), "blk") for owner in range(PANELS)
            )
            (first,) = multiply(left, jnp.where(mine == 0, chunk, right), weights)
            out = finish(out, start, chunk, first, first)
        return out[None], pivots

    raw = chunks[0]
    raw_far = lax.ppermute(raw, "blk", [(0, 2)])
    raw_middle = lax.ppermute(raw, "blk", [(1, 2)])
    lefts = []
    for chunk in chunks[1:]:
        lefts.append(lax.ppermute(chunk, "blk", [(0, 1)]))
    raw_near = lax.ppermute(raw, "blk", [(0, 1)])

    tops, raw = lax.optimization_barrier((jnp.stack(tops), raw))
    weights, top_out, pivots = factor(index, tops, own[:window], blocks - 1)
    out = lax.dynamic_update_slice(jnp.zeros_like(own), top_out, (0, 0))

    products = []
    for chunk, left in zip(chunks[1:], lefts):
        first, *updates = multiply(left, chunk, weights)
        moved = []
        for block, u in enumerate(updates, start=2):
            moved.append(lax.ppermute(u, "blk", [(1, block)]))
        products.append((first, moved))
        weights, _ = lax.optimization_barrier((weights, first))

    raw_left = jnp.where(mine == 2, raw_far, raw_near)
    raw_right = jnp.where(mine == 2, raw_middle, raw)
    raw_first, *updates = multiply(raw_left, raw_right, weights)
    update = jnp.where(mine == 2, raw_first, 0.0)
    for block in range(3, blocks):
        update += lax.ppermute(updates[block - 2], "blk", [(2, block)])
    out = finish(out, window, raw, raw_first, update)

    for start, chunk, (first, moved) in zip(starts[1:], chunks[1:], products):
        out = finish(out, start, chunk, first, sum(moved))
    return out[None], pivots


def solution(mesh):
    in_specs = (
        P("group", None, "blk"),
        P("group", "blk", None, None, None, None),
        P("group", "blk", None, None, None),
        P("group", "blk", None, None, None),
        P("group", "blk", None),
    )
    out_specs = (P("group", None, "blk"), P("group", None))
    return jax.shard_map(
        functools.partial(per_device, blocks=mesh.shape["blk"]),
        mesh=mesh,
        in_specs=in_specs,
        out_specs=out_specs,
        check_vma=False,
    )
```

profile of v0, /device:TPU:24, one launch (start us, length us, event | category | flops | bytes accessed | tf_op | source)
XLA Modules:
  0.0 300.1 jit_solution(13043197904083782511)
XLA Ops:
  3.2 4.6 %pack.1 = (f32[272,128]{1,0:T(8,128)}, f32[272,128]{1,0:T(8,128)}, f32[272,128]{1,0:T(8,128)}, f32[272,128]{1,0:T(8,128)}, f32[272,128]{1,0:T(8,128)}, /*index=5...) custom-call(s32[1,8]{1,0:T(1,128)} %bitcast.35, s32[8]{0:T(128)} %broadcast_xor_fusion.partners_ref, ...), custom_call_target="tpu_custom_call" | custom-call | tf_op jit(solution)/shard_map/pack/pallas_call | solution.py:62
  7.8 1.7 collective-permute-start.3
  12.8 1.8 collective-permute-done.3.refs_0_
  14.6 2.3 collective-permute-start.6
  18.8 2.2 collective-permute-done.5.refs_2_
  22.1 1.8 collective-permute-done.6.refs_3_
  24.0 3.0 collective-permute-done.8.refs_5_
  27.8 8.1 %assemble.1 = (f32[2048,128]{1,0:T(8,128)}, f32[512,128]{1,0:T(8,128)}, f32[1024,128]{1,0:T(8,128)}, f32[1024,128]{1,0:T(8,128)}, f32[1024,128]{1,0:T(8,128)}, /*index=5*/f32[1024,128]{1,0:T(8,128)}, f32[1024,128]{1,0:T(8,128)}) custom-call(s32[16,128]{1,0:T(8,128)} %convert_element_type.3.rows_ref, f32[8192,128]{1,0:T(8,128)} %bitcast.29, ...), custom_call_target="tpu_custom_call" | custom-call | tf_op jit(solution)/shard_map/assemble/pallas_call | solution.py:117
  38.0 1.5 collective-permute-start.16
  39.4 10.2 %collective-permute-start = (f32[256,128]{1,0:T(8,128)S(1)}, f32[256,128]{1,0:T(8,128)S(1)}, u32[]{:S(2)}, u32[]{:S(2)}) collective-permute-start(f32[256,128]{1,0:T(8,128)S(1)} %get-tuple-element.95), channel_id=1, source_target_pairs={{0,1},{1,2},{2,3},{3,0},{4,5},{5,6},{6,7},{7,4},{8,9},{9,10},{10,1... | collective-permute-start | bytes 393224 | tf_op jit(solution)/shard_map/ppermute | solution.py:318
  49.6 2.5 collective-permute-done
  52.8 1.5 collective-permute-start.17
  54.3 1.5 collective-permute-start.18
  57.3 1.6 collective-permute-start.10
  59.0 1.7 slice_bitcast_fusion.own_ref
  60.6 1.8 pad_maximum_fusion.tops_ref
  62.4 31.1 %factor.1 = (f32[3,256,128]{2,1,0:T(8,128)}, f32[512,128]{1,0:T(8,128)}, f32[1,256]{1,0:T(1,128)}) custom-call(s32[1]{0:T(128)} %bitcast.index_ref, f32[4,256,128]{2,1,0:T(8,128)} %pad_maximum_fusion.tops_ref, f32[512,128]{1,0:T(8,128)} %slice_bitcast_fusion.own_ref), custom_call_target="tpu_custom_call" | custom-call | tf_op jit(solution)/shard_map/factor/pallas_call | solution.py:245
  93.5 3.5 %multiply.7 = (f32[512,128]{1,0:T(8,128)}, f32[512,128]{1,0:T(8,128)}, f32[512,128]{1,0:T(8,128)}) custom-call(f32[512,128]{1,0:T(8,128)} %copy-done.18, f32[512,128]{1,0:T(8,128)} %get-tuple-element.61.right_ref, f32[3,256,128]{2,1,0:T(8,128)} %get-tuple-element.78.weights_ref), custom_call_target="tpu_custom_call" | custom-call | tf_op jit(solution)/shard_map/multiply/pallas_call | solution.py:272
  97.0 5.3 %multiply.8 = (f32[1024,128]{1,0:T(8,128)}, f32[1024,128]{1,0:T(8,128)}, f32[1024,128]{1,0:T(8,128)}) custom-call(f32[1024,128]{1,0:T(8,128)} %copy-done.14, f32[1024,128]{1,0:T(8,128)} %get-tuple-element.64.right_ref, f32[3,256,128]{2,1,0:T(8,128)} %get-tuple-element.78.weights_ref), custom_call_target="tpu_custom_call" | custom-call | tf_op jit(solution)/shard_map/multiply/pallas_call | solution.py:272
  102.3 5.3 %multiply.9 = (f32[1024,128]{1,0:T(8,128)}, f32[1024,128]{1,0:T(8,128)}, f32[1024,128]{1,0:T(8,128)}) custom-call(f32[1024,128]{1,0:T(8,128)} %copy-done.15, f32[1024,128]{1,0:T(8,128)} %get-tuple-element.67.right_ref, f32[3,256,128]{2,1,0:T(8,128)} %get-tuple-element.78.weights_ref), custom_call_target="tpu_custom_call" | custom-call | tf_op jit(solution)/shard_map/multiply/pallas_call | solution.py:272
  107.6 5.4 %multiply.10 = (f32[1024,128]{1,0:T(8,128)}, f32[1024,128]{1,0:T(8,128)}, f32[1024,128]{1,0:T(8,128)}) custom-call(f32[1024,128]{1,0:T(8,128)} %collective-permute-done.16.left_ref, f32[1024,128]{1,0:T(8,128)} %get-tuple-element.70.right_ref, f32[3,256,128]{2,1,0:T(8,128)} %get-tuple-element.78.weights_ref), custom_call_target="tpu_custom_call" | custom-call | tf_op jit(solution)/shard_map/multiply/pallas_call | solution.py:272
  113.0 5.3 %multiply.11 = (f32[1024,128]{1,0:T(8,128)}, f32[1024,128]{1,0:T(8,128)}, f32[1024,128]{1,0:T(8,128)}) custom-call(f32[1024,128]{1,0:T(8,128)} %collective-permute-done.17.left_ref, f32[1024,128]{1,0:T(8,128)} %get-tuple-element.73.right_ref, f32[3,256,128]{2,1,0:T(8,128)} %get-tuple-element.78.weights_ref), custom_call_target="tpu_custom_call" | custom-call | tf_op jit(solution)/shard_map/multiply/pallas_call | solution.py:272
  118.3 5.3 %multiply.12 = (f32[1024,128]{1,0:T(8,128)}, f32[1024,128]{1,0:T(8,128)}, f32[1024,128]{1,0:T(8,128)}) custom-call(f32[1024,128]{1,0:T(8,128)} %collective-permute-done.18.left_ref, f32[1024,128]{1,0:T(8,128)} %get-tuple-element.76.right_ref, f32[3,256,128]{2,1,0:T(8,128)} %get-tuple-element.78.weights_ref), custom_call_target="tpu_custom_call" | custom-call | tf_op jit(solution)/shard_map/multiply/pallas_call | solution.py:272
  125.9 9.1 %multiply.13 = (f32[2048,128]{1,0:T(8,128)}, f32[2048,128]{1,0:T(8,128)}, f32[2048,128]{1,0:T(8,128)}) custom-call(f32[2048,128]{1,0:T(8,128)} %broadcast_select_fusion.1.left_ref, f32[2048,128]{1,0:T(8,128)} %broadcast_select_fusion.right_ref, f32[3,256,128]{2,1,0:T(8,128)} %get-tuple-element.78.weights_ref), custom_call_target="tpu_custom_call" | custom-call | tf_op jit(solution)/shard_map/multiply/pallas_call | solution.py:272
  138.2 1.4 collective-permute-start.21
  141.6 65.4 %collective-permute-done.19 = f32[2048,128]{1,0:T(8,128)S(1)} collective-permute-done((f32[2048,128]{1,0:T(8,128)}, f32[2048,128]{1,0:T(8,128)S(1)}, u32[]{:S(2)}, u32[]{:S(2)}) %collective-permute-start.19) | collective-permute-done | bytes 1048608 | tf_op jit(solution)/shard_map/ppermute | solution.py:371
  207.9 1.4 collective-permute-start.25
  214.2 20.2 %collective-permute-done.25 = f32[1024,128]{1,0:T(8,128)S(1)} collective-permute-done((f32[1024,128]{1,0:T(8,128)S(1)}, f32[1024,128]{1,0:T(8,128)S(1)}, u32[]{:S(2)}, u32[]{:S(2)}) %collective-permute-start.25) | collective-permute-done | bytes 524320 | tf_op jit(solution)/shard_map/ppermute | solution.py:362
  236.5 20.3 %collective-permute-done.27 = f32[1024,128]{1,0:T(8,128)S(1)} collective-permute-done((f32[1024,128]{1,0:T(8,128)S(1)}, f32[1024,128]{1,0:T(8,128)S(1)}, u32[]{:S(2)}, u32[]{:S(2)}) %collective-permute-start.27) | collective-permute-done | bytes 524320 | tf_op jit(solution)/shard_map/ppermute | solution.py:362
  257.0 22.3 %collective-permute-done.29 = f32[1024,128]{1,0:T(8,128)S(1)} collective-permute-done((f32[1024,128]{1,0:T(8,128)S(1)}, f32[1024,128]{1,0:T(8,128)S(1)}, u32[]{:S(2)}, u32[]{:S(2)}) %collective-permute-start.29) | collective-permute-done | bytes 524320 | tf_op jit(solution)/shard_map/ppermute | solution.py:362
  279.5 18.5 %collective-permute-done.31 = f32[1024,128]{1,0:T(8,128)S(1)} collective-permute-done((f32[1024,128]{1,0:T(8,128)S(1)}, f32[1024,128]{1,0:T(8,128)S(1)}, u32[]{:S(2)}, u32[]{:S(2)}) %collective-permute-start.31) | collective-permute-done | bytes 524320 | tf_op jit(solution)/shard_map/ppermute | solution.py:362
  298.1 2.0 copy-done.1
  (142 shorter events, 29.3 us)
Async XLA Ops:
  1.6 36.4 %collective-permute-start.2 = (f32[256,128]{1,0:T(8,128)S(1)}, f32[256,128]{1,0:T(8,128)S(1)}, u32[]{:S(2)}, u32[]{:S(2)}) collective-permute-start(f32[256,128]{1,0:T(8,128)S(1)} %get-tuple-element.95), channel_id=1, source_target_pairs={{0,3},{1,0},{2,1},{3,2},{4,7},{5,4},{6,5},{7,6},{8,11},{9,8},{10,9... | collective-permute-start | bytes 393224 | tf_op jit(solution)/shard_map/ppermute | solution.py:318
  2.1 37.4 %collective-permute-start.1 = (f32[256,128]{1,0:T(8,128)S(1)}, f32[256,128]{1,0:T(8,128)}, u32[]{:S(2)}, u32[]{:S(2)}) collective-permute-start(f32[256,128]{1,0:T(8,128)S(1)} %get-tuple-element.95), channel_id=1, source_target_pairs={{0,2},{1,3},{2,0},{3,1},{4,6},{5,7},{6,4},{7,5},{8,10},{9,11},{10,... | collective-permute-start | bytes 393224 | tf_op jit(solution)/shard_map/ppermute | solution.py:318
  7.8 6.8 %collective-permute-start.3 = (f32[272,128]{1,0:T(8,128)}, f32[272,128]{1,0:T(8,128)S(1)}, u32[]{:S(2)}, u32[]{:S(2)}) collective-permute-start(f32[272,128]{1,0:T(8,128)} %get-tuple-element.48), channel_id=1, source_target_pairs={{0,28},{4,24},{8,20},{12,16},{16,12},{20,8},{24,4},{28,0},{1,29},{... | collective-permute-start | bytes 417800 | tf_op jit(solution)/shard_map/ppermute | solution.py:299
  9.5 8.5 %collective-permute-start.4 = (f32[272,128]{1,0:T(8,128)}, f32[272,128]{1,0:T(8,128)S(1)}, u32[]{:S(2)}, u32[]{:S(2)}) collective-permute-start(f32[272,128]{1,0:T(8,128)} %get-tuple-element.49), channel_id=1, source_target_pairs={{0,24},{4,28},{8,16},{12,20},{16,8},{20,12},{24,0},{28,4},{1,25},{... | collective-permute-start | bytes 417800 | tf_op jit(solution)/shard_map/ppermute | solution.py:299
  10.7 10.2 %collective-permute-start.5 = (f32[272,128]{1,0:T(8,128)}, f32[272,128]{1,0:T(8,128)S(1)}, u32[]{:S(2)}, u32[]{:S(2)}) collective-permute-start(f32[272,128]{1,0:T(8,128)} %get-tuple-element.50), channel_id=1, source_target_pairs={{0,20},{4,16},{8,28},{12,24},{16,4},{20,0},{24,12},{28,8},{1,21},{... | collective-permute-start | bytes 417800 | tf_op jit(solution)/shard_map/ppermute | solution.py:299
  14.6 9.3 %collective-permute-start.6 = (f32[272,128]{1,0:T(8,128)}, f32[272,128]{1,0:T(8,128)S(1)}, u32[]{:S(2)}, u32[]{:S(2)}) collective-permute-start(f32[272,128]{1,0:T(8,128)} %get-tuple-element.51), channel_id=1, source_target_pairs={{0,16},{4,20},{8,24},{12,28},{16,0},{20,4},{24,8},{28,12},{1,17},{... | collective-permute-start | bytes 417800 | tf_op jit(solution)/shard_map/ppermute | solution.py:299
  18.1 6.0 %collective-permute-start.7 = (f32[272,128]{1,0:T(8,128)}, f32[272,128]{1,0:T(8,128)S(1)}, u32[]{:S(2)}, u32[]{:S(2)}) collective-permute-start(f32[272,128]{1,0:T(8,128)} %get-tuple-element.52), channel_id=1, source_target_pairs={{0,12},{4,8},{8,4},{12,0},{16,28},{20,24},{24,20},{28,16},{1,13},{... | collective-permute-start | bytes 417800 | tf_op jit(solution)/shard_map/ppermute | solution.py:299
  20.9 6.1 %collective-permute-start.8 = (f32[272,128]{1,0:T(8,128)}, f32[272,128]{1,0:T(8,128)S(1)}, u32[]{:S(2)}, u32[]{:S(2)}) collective-permute-start(f32[272,128]{1,0:T(8,128)} %get-tuple-element.53), channel_id=1, source_target_pairs={{0,8},{4,12},{8,0},{12,4},{16,24},{20,28},{24,16},{28,20},{1,9},{5... | collective-permute-start | bytes 417800 | tf_op jit(solution)/shard_map/ppermute | solution.py:299
  23.9 3.1 %collective-permute-start.9 = (f32[272,128]{1,0:T(8,128)}, f32[272,128]{1,0:T(8,128)S(1)}, u32[]{:S(2)}, u32[]{:S(2)}) collective-permute-start(f32[272,128]{1,0:T(8,128)} %get-tuple-element.54), channel_id=1, source_target_pairs={{0,4},{4,0},{8,12},{12,8},{16,20},{20,16},{24,28},{28,24},{1,5},{5... | collective-permute-start | bytes 417800 | tf_op jit(solution)/shard_map/ppermute | solution.py:299
  35.8 18.5 %collective-permute-start.14 = (f32[1024,128]{1,0:T(8,128)}, f32[1024,128]{1,0:T(8,128)S(1)}, u32[]{:S(2)}, u32[]{:S(2)}) collective-permute-start(f32[1024,128]{1,0:T(8,128)} %get-tuple-element.64.right_ref), channel_id=1, source_target_pairs={{0,1},{4,5},{8,9},{12,13},{16,17},{20,21},{24,25},{28,29}} | collective-permute-start | bytes 1572872 | tf_op jit(solution)/shard_map/ppermute | solution.py:350
  36.5 87.1 %collective-permute-start.12 = (f32[2048,128]{1,0:T(8,128)}, f32[2048,128]{1,0:T(8,128)S(1)}, u32[]{:S(2)}, u32[]{:S(2)}) collective-permute-start(f32[2048,128]{1,0:T(8,128)} %get-tuple-element.59), channel_id=1, source_target_pairs={{1,2},{5,6},{9,10},{13,14},{17,18},{21,22},{25,26},{29,30}} | collective-permute-start | bytes 3145736 | tf_op jit(solution)/shard_map/ppermute | solution.py:347
  37.3 18.5 %collective-permute-start.15 = (f32[1024,128]{1,0:T(8,128)}, f32[1024,128]{1,0:T(8,128)S(1)}, u32[]{:S(2)}, u32[]{:S(2)}) collective-permute-start(f32[1024,128]{1,0:T(8,128)} %get-tuple-element.67.right_ref), channel_id=1, source_target_pairs={{0,1},{4,5},{8,9},{12,13},{16,17},{20,21},{24,25},{28,29}} | collective-permute-start | bytes 1572872 | tf_op jit(solution)/shard_map/ppermute | solution.py:350
  38.0 19.3 %collective-permute-start.16 = (f32[1024,128]{1,0:T(8,128)}, f32[1024,128]{1,0:T(8,128)}, u32[]{:S(2)}, u32[]{:S(2)}) collective-permute-start(f32[1024,128]{1,0:T(8,128)} %get-tuple-element.70.right_ref), channel_id=1, source_target_pairs={{0,1},{4,5},{8,9},{12,13},{16,17},{20,21},{24,25},{28,29}} | collective-permute-start | bytes 1572872 | tf_op jit(solution)/shard_map/ppermute | solution.py:350
  39.4 12.7 %collective-permute-start = (f32[256,128]{1,0:T(8,128)S(1)}, f32[256,128]{1,0:T(8,128)S(1)}, u32[]{:S(2)}, u32[]{:S(2)}) collective-permute-start(f32[256,128]{1,0:T(8,128)S(1)} %get-tuple-element.95), channel_id=1, source_target_pairs={{0,1},{1,2},{2,3},{3,0},{4,5},{5,6},{6,7},{7,4},{8,9},{9,10},{10,1... | collective-permute-start | bytes 393224 | tf_op jit(solution)/shard_map/ppermute | solution.py:318
  52.1 0.7 collective-permute-start.13
  52.8 60.2 %collective-permute-start.17 = (f32[1024,128]{1,0:T(8,128)}, f32[1024,128]{1,0:T(8,128)}, u32[]{:S(2)}, u32[]{:S(2)}) collective-permute-start(f32[1024,128]{1,0:T(8,128)} %get-tuple-element.73.right_ref), channel_id=1, source_target_pairs={{0,1},{4,5},{8,9},{12,13},{16,17},{20,21},{24,25},{28,29}} | collective-permute-start | bytes 1572872 | tf_op jit(solution)/shard_map/ppermute | solution.py:350
  54.3 64.0 %collective-permute-start.18 = (f32[1024,128]{1,0:T(8,128)}, f32[1024,128]{1,0:T(8,128)}, u32[]{:S(2)}, u32[]{:S(2)}) collective-permute-start(f32[1024,128]{1,0:T(8,128)} %get-tuple-element.76.right_ref), channel_id=1, source_target_pairs={{0,1},{4,5},{8,9},{12,13},{16,17},{20,21},{24,25},{28,29}} | collective-permute-start | bytes 1572872 | tf_op jit(solution)/shard_map/ppermute | solution.py:350
  56.6 68.2 %collective-permute-start.11 = (f32[2048,128]{1,0:T(8,128)}, f32[2048,128]{1,0:T(8,128)S(1)}, u32[]{:S(2)}, u32[]{:S(2)}) collective-permute-start(f32[2048,128]{1,0:T(8,128)} %get-tuple-element.59), channel_id=1, source_target_pairs={{0,1},{4,5},{8,9},{12,13},{16,17},{20,21},{24,25},{28,29}} | collective-permute-start | bytes 3145736 | tf_op jit(solution)/shard_map/ppermute | solution.py:351
  57.3 67.4 %collective-permute-start.10 = (f32[2048,128]{1,0:T(8,128)}, f32[2048,128]{1,0:T(8,128)}, u32[]{:S(2)}, u32[]{:S(2)}) collective-permute-start(f32[2048,128]{1,0:T(8,128)} %get-tuple-element.59), channel_id=1, source_target_pairs={{0,2},{4,6},{8,10},{12,14},{16,18},{20,22},{24,26},{28,30}} | collective-permute-start | bytes 3145736 | tf_op jit(solution)/shard_map/ppermute | solution.py:346
  135.0 72.0 %collective-permute-start.19 = (f32[2048,128]{1,0:T(8,128)}, f32[2048,128]{1,0:T(8,128)S(1)}, u32[]{:S(2)}, u32[]{:S(2)}) collective-permute-start(f32[2048,128]{1,0:T(8,128)} %get-tuple-element.80), channel_id=1, source_target_pairs={{2,3},{6,7},{10,11},{14,15},{18,19},{22,23},{26,27},{30,31}} | collective-permute-start | bytes 3145736 | tf_op jit(solution)/shard_map/ppermute | solution.py:371
  137.4 70.5 %collective-permute-start.20 = (f32[512,128]{1,0:T(8,128)S(1)}, f32[512,128]{1,0:T(8,128)S(1)}, u32[]{:S(2)}, u32[]{:S(2)}) collective-permute-start(f32[512,128]{1,0:T(8,128)S(1)} %copy-done.37), channel_id=1, source_target_pairs={{1,2},{5,6},{9,10},{13,14},{17,18},{21,22},{25,26},{29,30}} | collective-permute-start | bytes 786440 | tf_op jit(solution)/shard_map/ppermute | solution.py:362
  138.2 71.2 %collective-permute-start.21 = (f32[512,128]{1,0:T(8,128)S(1)}, f32[512,128]{1,0:T(8,128)S(1)}, u32[]{:S(2)}, u32[]{:S(2)}) collective-permute-start(f32[512,128]{1,0:T(8,128)S(1)} %copy-done.36), channel_id=1, source_target_pairs={{1,3},{5,7},{9,11},{13,15},{17,19},{21,23},{25,27},{29,31}} | collective-permute-start | bytes 786440 | tf_op jit(solution)/shard_map/ppermute | solution.py:362
  139.6 70.5 %collective-permute-start.22 = (f32[1024,128]{1,0:T(8,128)S(1)}, f32[1024,128]{1,0:T(8,128)S(1)}, u32[]{:S(2)}, u32[]{:S(2)}) collective-permute-start(f32[1024,128]{1,0:T(8,128)S(1)} %copy-done.35), channel_id=1, source_target_pairs={{1,2},{5,6},{9,10},{13,14},{17,18},{21,22},{25,26},{29,30}} | collective-permute-start | bytes 1572872 | tf_op jit(solution)/shard_map/ppermute | solution.py:362
  140.3 71.6 %collective-permute-start.23 = (f32[1024,128]{1,0:T(8,128)S(1)}, f32[1024,128]{1,0:T(8,128)S(1)}, u32[]{:S(2)}, u32[]{:S(2)}) collective-permute-start(f32[1024,128]{1,0:T(8,128)S(1)} %copy-done.34), channel_id=1, source_target_pairs={{1,3},{5,7},{9,11},{13,15},{17,19},{21,23},{25,27},{29,31}} | collective-permute-start | bytes 1572872 | tf_op jit(solution)/shard_map/ppermute | solution.py:362
  207.0 5.7 %collective-permute-start.24 = (f32[1024,128]{1,0:T(8,128)S(1)}, f32[1024,128]{1,0:T(8,128)S(1)}, u32[]{:S(2)}, u32[]{:S(2)}) collective-permute-start(f32[1024,128]{1,0:T(8,128)S(1)} %copy-done.33), channel_id=1, source_target_pairs={{1,2},{5,6},{9,10},{13,14},{17,18},{21,22},{25,26},{29,30}} | collective-permute-start | bytes 1572872 | tf_op jit(solution)/shard_map/ppermute | solution.py:362
  207.9 26.5 %collective-permute-start.25 = (f32[1024,128]{1,0:T(8,128)S(1)}, f32[1024,128]{1,0:T(8,128)S(1)}, u32[]{:S(2)}, u32[]{:S(2)}) collective-permute-start(f32[1024,128]{1,0:T(8,128)S(1)} %copy-done.32), channel_id=1, source_target_pairs={{1,3},{5,7},{9,11},{13,15},{17,19},{21,23},{25,27},{29,31}} | collective-permute-start | bytes 1572872 | tf_op jit(solution)/shard_map/ppermute | solution.py:362
  209.4 25.8 %collective-permute-start.26 = (f32[1024,128]{1,0:T(8,128)S(1)}, f32[1024,128]{1,0:T(8,128)S(1)}, u32[]{:S(2)}, u32[]{:S(2)}) collective-permute-start(f32[1024,128]{1,0:T(8,128)S(1)} %copy-done.31), channel_id=1, source_target_pairs={{1,2},{5,6},{9,10},{13,14},{17,18},{21,22},{25,26},{29,30}} | collective-permute-start | bytes 1572872 | tf_op jit(solution)/shard_map/ppermute | solution.py:362
  210.2 46.7 %collective-permute-start.27 = (f32[1024,128]{1,0:T(8,128)S(1)}, f32[1024,128]{1,0:T(8,128)S(1)}, u32[]{:S(2)}, u32[]{:S(2)}) collective-permute-start(f32[1024,128]{1,0:T(8,128)S(1)} %copy-done.30), channel_id=1, source_target_pairs={{1,3},{5,7},{9,11},{13,15},{17,19},{21,23},{25,27},{29,31}} | collective-permute-start | bytes 1572872 | tf_op jit(solution)/shard_map/ppermute | solution.py:362
  211.9 45.1 %collective-permute-start.28 = (f32[1024,128]{1,0:T(8,128)S(1)}, f32[1024,128]{1,0:T(8,128)S(1)}, u32[]{:S(2)}, u32[]{:S(2)}) collective-permute-start(f32[1024,128]{1,0:T(8,128)S(1)} %copy-done.29), channel_id=1, source_target_pairs={{1,2},{5,6},{9,10},{13,14},{17,18},{21,22},{25,26},{29,30}} | collective-permute-start | bytes 1572872 | tf_op jit(solution)/shard_map/ppermute | solution.py:362
  212.8 66.6 %collective-permute-start.29 = (f32[1024,128]{1,0:T(8,128)S(1)}, f32[1024,128]{1,0:T(8,128)S(1)}, u32[]{:S(2)}, u32[]{:S(2)}) collective-permute-start(f32[1024,128]{1,0:T(8,128)S(1)} %copy-done.28), channel_id=1, source_target_pairs={{1,3},{5,7},{9,11},{13,15},{17,19},{21,23},{25,27},{29,31}} | collective-permute-start | bytes 1572872 | tf_op jit(solution)/shard_map/ppermute | solution.py:362
  234.4 45.1 %collective-permute-start.30 = (f32[1024,128]{1,0:T(8,128)S(1)}, f32[1024,128]{1,0:T(8,128)S(1)}, u32[]{:S(2)}, u32[]{:S(2)}) collective-permute-start(f32[1024,128]{1,0:T(8,128)S(1)} %copy-done.27), channel_id=1, source_target_pairs={{1,2},{5,6},{9,10},{13,14},{17,18},{21,22},{25,26},{29,30}} | collective-permute-start | bytes 1572872 | tf_op jit(solution)/shard_map/ppermute | solution.py:362
  235.2 62.8 %collective-permute-start.31 = (f32[1024,128]{1,0:T(8,128)S(1)}, f32[1024,128]{1,0:T(8,128)S(1)}, u32[]{:S(2)}, u32[]{:S(2)}) collective-permute-start(f32[1024,128]{1,0:T(8,128)S(1)} %copy-done.26), channel_id=1, source_target_pairs={{1,3},{5,7},{9,11},{13,15},{17,19},{21,23},{25,27},{29,31}} | collective-permute-start | bytes 1572872 | tf_op jit(solution)/shard_map/ppermute | solution.py:362
  (38 other events, 1676.2 us)
where the time goes:
time: 301 us; the launch traced here: 300 us
  waiting for transfers between devices  159 us (53%)
  Pallas kernels  83 us (28%)
  starting transfers between devices  42.8 us (14%)
  local copies, waits for them, and re-layouts  7.06 us (2%)
  other arithmetic  6.53 us (2%)
    ppermute x12, waiting for transfers between devices, extend_and_factor(): moved.append(lax.ppermute(u, 'blk', [(1, block)]))  81.6 us
    ppermute x1, waiting for transfers between devices, extend_and_factor(): update += lax.ppermute(updates[block - 2], 'blk', [(2, block)])  65.4 us
    pallas_call x7, Pallas kernels, multiply(): pl.pallas_call(multiply_kernel, grid=(rows // tile,), in_specs=[spec, spe...  39.3 us
    pallas_call x1, Pallas kernels, factor(): pl.pallas_call(factor_kernel, in_specs=[SMEM, VMEM, VMEM], out_specs=[VME...  31.1 us
    ppermute x12, starting transfers between devices, extend_and_factor(): moved.append(lax.ppermute(u, 'blk', [(1, block)]))  12.5 us
    ppermute x3, starting transfers between devices, extend_and_factor(): tops.append(lax.ppermute(top, 'blk', pairs))  10.7 us
    ppermute x7, waiting for transfers between devices, exchange(): got.append(lax.ppermute(block, 'group', pairs))  9.85 us
    ppermute x7, starting transfers between devices, exchange(): got.append(lax.ppermute(block, 'group', pairs))  8.65 us
  transfers between devices with their start and end apart: 32, of which 12 were waited for; matrix products, arithmetic and copies ran while one was open for 3% of the time, Pallas kernels for 25%

commit v1 on v0

--- a/solution.py
+++ b/solution.py
@@ -13,9 +13,18 @@
 VMEM = pl.BlockSpec(memory_space=pltpu.VMEM)
 SMEM = pl.BlockSpec(memory_space=pltpu.SMEM)
 ANY = pl.BlockSpec(memory_space=pl.ANY)
+HBM = pl.BlockSpec(memory_space=pltpu.HBM)
 RAW_ROWS = 2048
 FIRST_ROWS = 512
 CHUNKS = 6
+
+
+def grant(mib):
+    return pltpu.CompilerParams(vmem_limit_bytes=mib << 20)
+
+
+def in_hbm(x):
+    return pltpu.with_memory_space_constraint(x, pltpu.HBM)
 
 
 def dot(a, b, lhs=1, rhs=0):
@@ -24,24 +33,29 @@
     )
 
 
-def pack_kernel(counts_ref, partners_ref, blocks_ref, rows_ref, cols_ref, *refs):
-    send_refs, (staged_ref, sem) = refs[:-2], refs[-2:]
+def pack_kernel(index_ref, blocks_hbm, rows_hbm, cols_hbm, counts_hbm, *refs, distances):
+    send_refs, (staged_ref, rows_ref, cols_ref, counts_ref, sem) = refs[:-5], refs[-5:]
     slots, width = rows_ref.shape[1], rows_ref.shape[2]
     target_ids = lax.broadcasted_iota(jnp.int32, (width, width), 0)
+    partners = [index_ref[0] ^ distance for distance in distances]
+    count = len(distances)
+    small = [(counts_hbm, counts_ref), (cols_hbm, cols_ref), (rows_hbm, rows_ref)]
+    small = [pltpu.make_async_copy(*pair, sem.at[count + i]) for i, pair in enumerate(small)]
     copies = [
-        pltpu.make_async_copy(blocks_ref.at[partners_ref[k]], staged_ref.at[k], sem.at[k])
-        for k in range(len(send_refs))
+        pltpu.make_async_copy(blocks_hbm.at[partner], staged_ref.at[k], sem.at[k])
+        for k, partner in enumerate(partners)
     ]
-    for copy in copies:
+    for copy in small + copies:
         copy.start()
-    for k, send_ref in enumerate(send_refs):
-        partner = partners_ref[k]
+    for copy in small:
+        copy.wait()
+    for k, (partner, send_ref) in enumerate(zip(partners, send_refs)):
         copies[k].wait()
         live_slots = counts_ref[0, partner]
-        indices = jnp.concatenate([rows_ref[partner], cols_ref[partner]], axis=0)
+        rows, columns = rows_ref[partner], cols_ref[partner]
         for slot in range(slots):
-            columns = jnp.broadcast_to(indices[slots + slot : slots + slot + 1, :], (width, width))
-            placement = (columns == target_ids).astype(jnp.float32).astype(jnp.bfloat16)
+            placement = jnp.broadcast_to(columns[slot : slot + 1, :], (width, width)) == target_ids
+            placement = placement.astype(jnp.float32).astype(jnp.bfloat16)
             left = staged_ref[k, slot]
             placed = jnp.zeros((width, width), jnp.float32)
             for _ in range(3):
@@ -53,80 +67,82 @@
             live = jnp.full((width, width), slot < live_slots)
             base = slot * (width + 8)
             send_ref[base : base + width, :] = jnp.where(live, placed, jnp.zeros_like(placed))
-            row_ids = indices[slot : slot + 1, :].astype(jnp.float32)
+            row_ids = rows[slot : slot + 1, :].astype(jnp.float32)
             send_ref[base + width : base + width + 8, :] = jnp.broadcast_to(row_ids, (8, width))
 
 
-def pack(blocks, rows, cols, counts, partners):
-    groups, slots, width = rows.shape
+def pack(blocks, rows, cols, counts, index, distances):
+    slots, width = rows.shape[1:]
+    count = len(distances)
     return pl.pallas_call(
-        pack_kernel,
-        in_specs=[SMEM, SMEM, ANY, VMEM, VMEM],
-        out_specs=[VMEM] * groups,
-        out_shape=[jax.ShapeDtypeStruct((slots * (width + 8), width), jnp.float32)] * groups,
+        functools.partial(pack_kernel, distances=distances),
+        in_specs=[SMEM] + [HBM] * 4,
+        out_specs=[VMEM] * count,
+        out_shape=[jax.ShapeDtypeStruct((slots * (width + 8), width), jnp.float32)] * count,
         scratch_shapes=[
-            pltpu.VMEM(blocks.shape, jnp.float32),
-            pltpu.SemaphoreType.DMA((groups,)),
+            pltpu.VMEM((count,) + blocks.shape[1:], jnp.float32),
+            pltpu.VMEM(rows.shape, jnp.int32),
+            pltpu.VMEM(cols.shape, jnp.int32),
+            pltpu.SMEM(counts.shape, jnp.int32),
+            pltpu.SemaphoreType.DMA((count + 3,)),
         ],
+        compiler_params=grant(8),
         name="pack",
-    )(counts, partners, blocks, rows, cols)
-
-
-def assemble_kernel(rows_ref, front_ref, *refs, window, sources, starts):
-    block_refs, out_refs = refs[:sources], refs[sources:-4]
-    sums_ref, staged_ref, front_sem, sem = refs[-4:]
-    width = staged_ref.shape[2]
-    height = width + 8
-    slots = staged_ref.shape[1] // height
-    rest = front_ref.shape[0] - window
+    )(index, *(in_hbm(x) for x in (blocks, rows, cols, counts)))
+
+
+def assemble_kernel(rows_ref, front_ref, *refs, window, sources):
+    block_refs, out_refs, (sums_ref, sem) = refs[:sources], refs[sources:-2], refs[-2:]
+    width = rows_ref.shape[1]
+    slots = rows_ref.shape[0] // sources
     batch = 16
-    loads = [pltpu.make_async_copy(front_ref.at[pl.ds(window, rest)], sums_ref, front_sem)]
-    loads += [
-        pltpu.make_async_copy(ref, staged_ref.at[i], sem.at[i]) for i, ref in enumerate(block_refs)
-    ]
-    for copy in loads:
-        copy.start()
-    for copy in loads:
-        copy.wait()
-
-    def add_block(block, carry):
-        source, base = block // slots, lax.rem(block, slots) * height
+    load = pltpu.make_async_copy(front_ref.at[pl.ds(window, sums_ref.shape[0])], sums_ref, sem.at[0])
+    load.start()
+    load.wait()
+
+    def add_slot(block_ref, block, base):
         for first in range(0, width, batch):
             targets = [rows_ref[block, first + i] - window for i in range(batch)]
             sums = [
-                sums_ref[pl.ds(targets[i], 1), :] + staged_ref[source, pl.ds(base + first + i, 1), :]
+                sums_ref[pl.ds(targets[i], 1), :] + block_ref[pl.ds(base + first + i, 1), :]
                 for i in range(batch)
             ]
             for i in range(batch):
                 sums_ref[pl.ds(targets[i], 1), :] = sums[i]
-        return carry
-
-    lax.fori_loop(0, sources * slots, add_block, 0)
-    stores = [
-        pltpu.make_async_copy(sums_ref.at[pl.ds(start - window, ref.shape[0])], ref, sem.at[i])
-        for i, (start, ref) in enumerate(zip(starts, out_refs))
-    ]
-    for copy in stores:
+
+    for source, block_ref in enumerate(block_refs):
+
+        def add(slot, carry):
+            add_slot(block_ref, source * slots + slot, slot * (width + 8))
+            return carry
+
+        lax.fori_loop(0, slots, add, 0)
+    copies, first = [], 0
+    for i, ref in enumerate(out_refs):
+        rows = pl.ds(first, ref.shape[0])
+        copies.append(pltpu.make_async_copy(sums_ref.at[rows], ref, sem.at[i]))
+        first += ref.shape[0]
+    for copy in copies:
         copy.start()
-    for copy in stores:
+    for copy in copies:
         copy.wait()
 
 
-def assemble(rows, blocks, front, window, starts, sizes):
+def assemble(rows, blocks, front, window, sizes):
     width = front.shape[1]
+    held = [pltpu.with_memory_space_constraint(x, pltpu.VMEM) for x in blocks]
     return pl.pallas_call(
-        functools.partial(assemble_kernel, window=window, sources=len(blocks), starts=starts),
-        in_specs=[SMEM] + [ANY] * (1 + len(blocks)),
-        out_specs=[ANY] * len(sizes),
-        out_shape=[jax.ShapeDtypeStruct((size, width), jnp.float32) for size in sizes],
+        functools.partial(assemble_kernel, window=window, sources=len(blocks)),
+        in_specs=[SMEM, HBM] + [VMEM] * len(held),
+        out_specs=[HBM] * len(sizes),
+        out_shape=[pltpu.HBM((size, width), jnp.float32) for size in sizes],
         scratch_shapes=[
             pltpu.VMEM((front.shape[0] - window, width), jnp.float32),
-            pltpu.VMEM((len(blocks),) + blocks[0].shape, jnp.float32),
-            pltpu.SemaphoreType.DMA,
-            pltpu.SemaphoreType.DMA((max(len(blocks), len(sizes)),)),
+            pltpu.SemaphoreType.DMA((len(sizes),)),
         ],
+        compiler_params=grant(6),
         name="assemble",
-    )(rows, front, *blocks)
+    )(rows, in_hbm(front), *held)
 
 
 def eliminate(m_ref, e_ref, wt_ref):
@@ -163,7 +179,7 @@
 
 
 def factor_kernel(
-    index_ref, tops_ref, own_ref, weights_ref, top_out_ref, pivots_ref, m_ref, e_ref, wt_ref, g_ref, h_ref
+    index_ref, tops_ref, own_ref, weights_ref, out_ref, pivots_ref, m_ref, e_ref, wt_ref, g_ref, h_ref
 ):
     blocks, width = tops_ref.shape[0], tops_ref.shape[2]
     mine = index_ref[0]
@@ -224,36 +240,42 @@
 
         @pl.when(mine <= 1)
         def _():
-            top_out_ref[rows, :] = g_ref[mine, block].T
+            out_ref[rows, :] = g_ref[mine, block].T
 
         @pl.when(mine > 1)
         def _():
             update = dot(g_ref[0, block], h_ref[0, mine], 0, 0)
             update += dot(g_ref[1, block], h_ref[1, mine], 0, 0)
-            top_out_ref[rows, :] = own_ref[rows, :] - update
+            out_ref[rows, :] = own_ref[rows, :] - update
 
         return carry
 
     lax.fori_loop(0, blocks, top_rows, 0)
 
 
-def factor(index, tops, own_top, slots):
+def factor(index, tops, own, slots):
     blocks, _, width = tops.shape
     window = blocks * width
+    window_spec = pl.BlockSpec((window, width), lambda i: (0, 0))
+    tops_spec = pl.BlockSpec(tops.shape, lambda i: (0, 0, 0))
+    weights_spec = pl.BlockSpec((slots, 2 * width, width), lambda i: (0, 0, 0))
+    pivots_spec = pl.BlockSpec((1, 2 * width), lambda i: (0, 0))
     square = pltpu.VMEM((width, width), jnp.float32)
     panels = pltpu.VMEM((PANELS, blocks, width, width), jnp.float32)
     return pl.pallas_call(
         factor_kernel,
-        in_specs=[SMEM, VMEM, VMEM],
-        out_specs=[VMEM, VMEM, VMEM],
+        grid=(1,),
+        in_specs=[SMEM, tops_spec, window_spec],
+        out_specs=[weights_spec, window_spec, pivots_spec],
         out_shape=[
             jax.ShapeDtypeStruct((slots, 2 * width, width), jnp.float32),
-            jax.ShapeDtypeStruct((window, width), jnp.float32),
+            jax.ShapeDtypeStruct(own.shape, jnp.float32),
             jax.ShapeDtypeStruct((1, 2 * width), jnp.float32),
         ],
         scratch_shapes=[square, square, square, panels, panels],
+        compiler_params=grant(24),
         name="factor",
-    )(index, tops, own_top)
+    )(index, tops, own)
 
 
 def multiply_kernel(left_ref, right_ref, weights_ref, *out_refs):
@@ -275,8 +297,41 @@
         in_specs=[spec, spec, pl.BlockSpec(weights.shape, lambda i: (0, 0, 0))],
         out_specs=[spec] * count,
         out_shape=[jax.ShapeDtypeStruct((rows, width), jnp.float32)] * count,
+        compiler_params=grant(12),
         name="multiply",
     )(left, right, weights)
+
+
+def finish_kernel(index_ref, own_ref, first_ref, *refs):
+    update_refs, out_ref = refs[:-2], refs[-1]
+
+    @pl.when(index_ref[0] < PANELS)
+    def _():
+        out_ref[...] = first_ref[...]
+
+    @pl.when(index_ref[0] >= PANELS)
+    def _():
+        rows = own_ref[...]
+        for update_ref in update_refs:
+            rows = rows - update_ref[...]
+        out_ref[...] = rows
+
+
+def finish(index, out, start, own_rows, first, updates):
+    rows, width = own_rows.shape
+    tile = 256
+    spec = pl.BlockSpec((tile, width), lambda i: (i, 0))
+    count = 2 + len(updates)
+    return pl.pallas_call(
+        finish_kernel,
+        grid=(rows // tile,),
+        in_specs=[SMEM] + [spec] * count + [ANY],
+        out_specs=pl.BlockSpec((tile, width), lambda i: (start // tile + i, 0)),
+        out_shape=pltpu.HBM(out.shape, jnp.float32),
+        input_output_aliases={count + 1: 0},
+        compiler_params=grant(6),
+        name="finish",
+    )(index, own_rows, first, *updates, in_hbm(out))
 
 
 def cut_rows(first, last):
@@ -289,17 +344,6 @@
     return [first + sum(sizes[:i]) for i in range(len(sizes))], sizes
 
 
-def exchange(packed, groups):
-    got = []
-    for distance, block in packed:
-        if distance == 0:
-            got.append(block)
-            continue
-        pairs = [(i, i ^ distance) for i in range(groups)]
-        got.append(lax.ppermute(block, "group", pairs))
-    return got
-
-
 def per_device(front, child_blocks, child_rows, child_cols, child_counts, *, blocks):
     return extend_and_factor(front[0], child_blocks[0, 0], child_rows[0, 0], child_cols[0, 0], child_counts[0], blocks)
 
@@ -317,29 +361,30 @@
         pairs = [(i, (i + shift) % blocks) for i in range(blocks)]
         tops.append(lax.ppermute(top, "blk", pairs))
 
+    group = lax.axis_index("group").astype(jnp.int32).reshape(1)
     distances = sorted(range(groups), key=lambda d: (-bin(d >> 1).count("1"), -d))
-    partners = jnp.array(distances, jnp.int32) ^ lax.axis_index("group").astype(jnp.int32)
-    packed = pack(child_blocks, child_rows, child_cols, child_counts, partners)
-    got = exchange(list(zip(distances, packed)), groups)
+    got = []
+    for part in [distances[:2], distances[2:]]:
+        packed = pack(child_blocks, child_rows, child_cols, child_counts, group, part)
+        for distance, block in zip(part, packed):
+            if distance > 0:
+                pairs = [(i, i ^ distance) for i in range(groups)]
+                block = lax.ppermute(block, "group", pairs)
+            got.append(block)
     row_lines = [slot * (width + 8) + width for slot in range(slots)]
     rows = jnp.concatenate([g[i : i + 1] for g in got for i in row_lines]).astype(jnp.int32)
     starts, sizes = cut_rows(window, total)
-    chunks = assemble(rows, got, own, window, starts, sizes)
-
-    def finish(out, start, own_rows, first, update):
-        mixed = jnp.where(mine <= 1, first, own_rows - update)
-        return lax.dynamic_update_slice(out, mixed, (start, 0))
+    chunks = assemble(rows, got, own, window, sizes)
 
     if blocks > 4:
-        weights, top_out, pivots = factor(index, jnp.stack(tops), own[:window], 1)
-        out = lax.dynamic_update_slice(jnp.zeros_like(own), top_out, (0, 0))
+        weights, out, pivots = factor(index, jnp.stack(tops), own, 1)
         for start, chunk in zip(starts, chunks):
             out, chunk = lax.optimization_barrier((out, chunk))
             left, right = (
                 lax.psum(jnp.where(mine == owner, chunk, 0.0), "blk") for owner in range(PANELS)
             )
             (first,) = multiply(left, jnp.where(mine == 0, chunk, right), weights)
-            out = finish(out, start, chunk, first, first)
+            out = finish(index, out, start, chunk, first, [first])
         return out[None], pivots
 
     raw = chunks[0]
@@ -351,8 +396,7 @@
     raw_near = lax.ppermute(raw, "blk", [(0, 1)])
 
     tops, raw = lax.optimization_barrier((jnp.stack(tops), raw))
-    weights, top_out, pivots = factor(index, tops, own[:window], blocks - 1)
-    out = lax.dynamic_update_slice(jnp.zeros_like(own), top_out, (0, 0))
+    weights, out, pivots = factor(index, tops, own, blocks - 1)
 
     products = []
     for chunk, left in zip(chunks[1:], lefts):
@@ -366,13 +410,13 @@
     raw_left = jnp.where(mine == 2, raw_far, raw_near)
     raw_right = jnp.where(mine == 2, raw_middle, raw)
     raw_first, *updates = multiply(raw_left, raw_right, weights)
-    update = jnp.where(mine == 2, raw_first, 0.0)
+    moved = [jnp.where(mine == 2, raw_first, 0.0)]
     for block in range(3, blocks):
-        update += lax.ppermute(updates[block - 2], "blk", [(2, block)])
-    out = finish(out, window, raw, raw_first, update)
+        moved.append(lax.ppermute(updates[block - 2], "blk", [(2, block)]))
+    out = finish(index, out, window, raw, raw_first, moved)
 
     for start, chunk, (first, moved) in zip(starts[1:], chunks[1:], products):
-        out = finish(out, start, chunk, first, sum(moved))
+        out = finish(index, out, start, chunk, first, moved)
     return out[None], pivots
 
 

time: 301 us -> 279 us (0.927)
  waiting for transfers between devices: 159 us -> 151 us
  Pallas kernels: 83 us -> 77.4 us
  other arithmetic: 6.53 us -> 2.62 us
  local copies, waits for them, and re-layouts: 7.06 us -> 3.2 us
    ppermute x8, waiting for transfers between devices: 75.2 us -> 7.73 us  [the longest x7 7.72 us: extend_and_factor(): block = lax.ppermute(block, 'group', pairs)]
    ppermute x12, waiting for transfers between devices: 81.6 us -> 141 us  [extend_and_factor(): moved.append(lax.ppermute(u, 'blk', [(1, block)]))]
    pallas_call x7, Pallas kernels: 39.3 us -> 25.5 us  [multiply(): pl.pallas_call(multiply_kernel, grid=(rows // tile,), in_specs=[spec, spe...]
    pallas_call x2 -> x10, Pallas kernels: 35.6 us -> 44.4 us  [the longest x1 29.8 us: factor(): pl.pallas_call(factor_kernel, grid=(1,), in_specs=[SMEM, tops_spec, windo...]
  transfers between devices with their start and end apart: 32 -> 32, of which waited for: 12 -> 11; matrix products, arithmetic and copies ran while one was open for 3% -> 1% of each run, Pallas kernels for 25% -> 27%
where the time goes in v1:
time: 279 us; the launch traced here: 278 us
  waiting for transfers between devices  151 us (54%)
  Pallas kernels  77.4 us (28%)
  starting transfers between devices  42.4 us (15%)
  local copies, waits for them, and re-layouts  3.2 us (1%)
    ppermute x12, waiting for transfers between devices, extend_and_factor(): moved.append(lax.ppermute(u, 'blk', [(1, block)]))  141 us
    pallas_call x1, Pallas kernels, factor(): pl.pallas_call(factor_kernel, grid=(1,), in_specs=[SMEM, tops_spec, windo...  29.8 us
    pallas_call x7, Pallas kernels, multiply(): pl.pallas_call(multiply_kernel, grid=(rows // tile,), in_specs=[spec, spe...  25.5 us
    ppermute x12, starting transfers between devices, extend_and_factor(): moved.append(lax.ppermute(u, 'blk', [(1, block)]))  12 us
    ppermute x3, starting transfers between devices, extend_and_factor(): tops.append(lax.ppermute(top, 'blk', pairs))  10.7 us
    pallas_call x7, Pallas kernels, finish(): pl.pallas_call(finish_kernel, grid=(rows // tile,), in_specs=[SMEM] + [sp...  10.5 us
    ppermute x7, starting transfers between devices, extend_and_factor(): block = lax.ppermute(block, 'group', pairs)  8.47 us
    ppermute x7, waiting for transfers between devices, extend_and_factor(): block = lax.ppermute(block, 'group', pairs)  7.72 us
  transfers between devices with their start and end apart: 32, of which 11 were waited for; matrix products, arithmetic and copies ran while one was open for 1% of the time, Pallas kernels for 27%

profile of v1, /device:TPU:24, one launch (start us, length us, event | category | flops | bytes accessed | tf_op | source)
XLA Modules:
  0.0 278.0 jit_solution(7698946979946572586)
XLA Ops:
  2.1 1.5 pack.2
  3.6 1.7 collective-permute-start
  6.5 2.6 pack.3
  9.1 1.4 collective-permute-start.2
  10.6 1.8 collective-permute-start.3
  14.6 1.9 collective-permute-done.2.refs_2_
  17.7 1.8 collective-permute-done.3.refs_3_
  19.6 2.8 %collective-permute-done.5.refs_5_ = f32[272,128]{1,0:T(8,128)S(1)} collective-permute-done((f32[272,128]{1,0:T(8,128)S(1)}, f32[272,128]{1,0:T(8,128)S(1)}, u32[]{:S(2)}, u32[]{:S(2)}) %collective-permute-start.5) | collective-permute-done | bytes 139296 | tf_op jit(solution)/shard_map/ppermute | solution.py:372
  22.5 7.4 %assemble.1 = (f32[2048,128]{1,0:T(8,128)}, f32[512,128]{1,0:T(8,128)}, f32[1024,128]{1,0:T(8,128)}, f32[1024,128]{1,0:T(8,128)}, f32[1024,128]{1,0:T(8,128)}, /*index=5*/f32[1024,128]{1,0:T(8,128)}, f32[1024,128]{1,0:T(8,128)}) custom-call(s32[16,128]{1,0:T(8,128)S(1)} %convert_element_type.3.rows_ref, f32[8192,128]{1,0:T(8,128)} %bitcast.13, ...), custom_call_target="tpu_custom_call" | custom-call | tf_op jit(solution)/shard_map/assemble/pallas_call | solution.py:134
  30.8 1.7 collective-permute-start.30
  33.8 10.2 %collective-permute-start.8 = (f32[256,128]{1,0:T(8,128)S(1)}, f32[256,128]{1,0:T(8,128)}, u32[]{:S(2)}, u32[]{:S(2)}) collective-permute-start(f32[256,128]{1,0:T(8,128)S(1)} %get-tuple-element.95), channel_id=1, source_target_pairs={{0,1},{1,2},{2,3},{3,0},{4,5},{5,6},{6,7},{7,4},{8,9},{9,10},{10,1... | collective-permute-start | bytes 393224 | tf_op jit(solution)/shard_map/ppermute | solution.py:362
  44.0 2.5 collective-permute-done.8
  47.9 1.5 collective-permute-start.7
  49.4 1.6 collective-permute-start.29
  51.0 1.6 collective-permute-start.28
  53.7 2.2 copy-done
  55.9 29.8 %factor.1 = (f32[3,256,128]{2,1,0:T(8,128)S(1)}, f32[8192,128]{1,0:T(8,128)}, f32[1,256]{1,0:T(1,128)}) custom-call(s32[1]{0:T(128)} %bitcast.index_ref, f32[4,256,128]{2,1,0:T(8,128)S(1)} %pad_maximum_fusion.tops_ref, f32[8192,128]{1,0:T(8,128)S(1)} %bitcast.14), custom_call_target="tpu_custom_call" | custom-call | tf_op jit(solution)/shard_map/factor/pallas_call | solution.py:265
  85.7 1.6 multiply.7
  87.3 3.2 %multiply.8 = (f32[1024,128]{1,0:T(8,128)S(1)}, f32[1024,128]{1,0:T(8,128)S(1)}, f32[1024,128]{1,0:T(8,128)S(1)}) custom-call(f32[1024,128]{1,0:T(8,128)S(1)} %collective-permute-done.12.left_ref, f32[1024,128]{1,0:T(8,128)S(1)} %copy-done.6, f32[3,256,128]{2,1,0:T(8,128)S(1)} %get-tuple-element.89.weights_ref), custom_call_target="tpu_custom_call" | custom-call | tf_op jit(solution)/shard_map/multiply/pallas_call | solution.py:294
  90.5 3.2 %multiply.9 = (f32[1024,128]{1,0:T(8,128)S(1)}, f32[1024,128]{1,0:T(8,128)S(1)}, f32[1024,128]{1,0:T(8,128)S(1)}) custom-call(f32[1024,128]{1,0:T(8,128)S(1)} %collective-permute-done.13.left_ref, f32[1024,128]{1,0:T(8,128)S(1)} %copy-done.5, f32[3,256,128]{2,1,0:T(8,128)S(1)} %get-tuple-element.89.weights_ref), custom_call_target="tpu_custom_call" | custom-call | tf_op jit(solution)/shard_map/multiply/pallas_call | solution.py:294
  93.7 3.2 %multiply.10 = (f32[1024,128]{1,0:T(8,128)S(1)}, f32[1024,128]{1,0:T(8,128)S(1)}, f32[1024,128]{1,0:T(8,128)S(1)}) custom-call(f32[1024,128]{1,0:T(8,128)S(1)} %collective-permute-done.14.left_ref, f32[1024,128]{1,0:T(8,128)S(1)} %copy-done.4, f32[3,256,128]{2,1,0:T(8,128)S(1)} %get-tuple-element.89.weights_ref), custom_call_target="tpu_custom_call" | custom-call | tf_op jit(solution)/shard_map/multiply/pallas_call | solution.py:294
  97.8 3.2 %multiply.11 = (f32[1024,128]{1,0:T(8,128)S(1)}, f32[1024,128]{1,0:T(8,128)S(1)}, f32[1024,128]{1,0:T(8,128)S(1)}) custom-call(f32[1024,128]{1,0:T(8,128)S(1)} %collective-permute-done.15.left_ref, f32[1024,128]{1,0:T(8,128)S(1)} %copy-done.3, f32[3,256,128]{2,1,0:T(8,128)S(1)} %get-tuple-element.89.weights_ref), custom_call_target="tpu_custom_call" | custom-call | tf_op jit(solution)/shard_map/multiply/pallas_call | solution.py:294
  101.0 4.2 %multiply.12 = (f32[1024,128]{1,0:T(8,128)S(1)}, f32[1024,128]{1,0:T(8,128)S(1)}, f32[1024,128]{1,0:T(8,128)S(1)}) custom-call(f32[1024,128]{1,0:T(8,128)} %collective-permute-done.7.left_ref, f32[1024,128]{1,0:T(8,128)S(1)} %copy-done.2, f32[3,256,128]{2,1,0:T(8,128)S(1)} %get-tuple-element.89.weights_ref), custom_call_target="tpu_custom_call" | custom-call | tf_op jit(solution)/shard_map/multiply/pallas_call | solution.py:294
  106.8 7.0 %multiply.13 = (f32[2048,128]{1,0:T(8,128)S(1)}, f32[2048,128]{1,0:T(8,128)}, f32[2048,128]{1,0:T(8,128)S(1)}) custom-call(f32[2048,128]{1,0:T(8,128)S(1)} %broadcast_select_fusion.2.left_ref, f32[2048,128]{1,0:T(8,128)S(1)} %broadcast_select_fusion.1.right_ref, f32[3,256,128]{2,1,0:T(8,128)S(1)} %get-tuple-element.89.weights_ref), custom_call_target="tpu_custom_call" | custom-call | tf_op jit(solution)/shard_map/multiply/pallas_call | solution.py:294
  119.1 60.3 %collective-permute-done.27.refs_1_ = f32[512,128]{1,0:T(8,128)S(1)} collective-permute-done((f32[512,128]{1,0:T(8,128)S(1)}, f32[512,128]{1,0:T(8,128)S(1)}, u32[]{:S(2)}, u32[]{:S(2)}) %collective-permute-start.27) | collective-permute-done | bytes 262176 | tf_op jit(solution)/shard_map/ppermute | solution.py:406
  181.3 9.2 %collective-permute-done.25.refs_1_ = f32[1024,128]{1,0:T(8,128)S(1)} collective-permute-done((f32[1024,128]{1,0:T(8,128)S(1)}, f32[1024,128]{1,0:T(8,128)S(1)}, u32[]{:S(2)}, u32[]{:S(2)}) %collective-permute-start.25) | collective-permute-done | bytes 524320 | tf_op jit(solution)/shard_map/ppermute | solution.py:406
  192.6 20.5 %collective-permute-done.23.refs_1_ = f32[1024,128]{1,0:T(8,128)S(1)} collective-permute-done((f32[1024,128]{1,0:T(8,128)S(1)}, f32[1024,128]{1,0:T(8,128)S(1)}, u32[]{:S(2)}, u32[]{:S(2)}) %collective-permute-start.23) | collective-permute-done | bytes 524320 | tf_op jit(solution)/shard_map/ppermute | solution.py:406
  216.5 2.8 %finish.7.refs_2_ = f32[8192,128]{1,0:T(8,128)} custom-call(s32[1]{0:T(128)} %bitcast.index_ref, f32[2048,128]{1,0:T(8,128)S(1)} %copy-done.1, f32[2048,128]{1,0:T(8,128)S(1)} %get-tuple-element.90.first_ref, f32[2048,128]{1,0:T(8,128)S(1)} %broadcast_select_fusion.refs_0_, ...), custom_call_target="tpu_custom_call", output_to_operand_aliasing={{}: (5, {})} | custom-call | tf_op jit(solution)/shard_map/finish/pallas_call | solution.py:325
  222.8 12.8 %collective-permute-done.21.refs_1_ = f32[1024,128]{1,0:T(8,128)S(1)} collective-permute-done((f32[1024,128]{1,0:T(8,128)S(1)}, f32[1024,128]{1,0:T(8,128)S(1)}, u32[]{:S(2)}, u32[]{:S(2)}) %collective-permute-start.21) | collective-permute-done | bytes 524320 | tf_op jit(solution)/shard_map/ppermute | solution.py:406
  236.9 21.1 %collective-permute-done.19.refs_1_ = f32[1024,128]{1,0:T(8,128)S(1)} collective-permute-done((f32[1024,128]{1,0:T(8,128)S(1)}, f32[1024,128]{1,0:T(8,128)S(1)}, u32[]{:S(2)}, u32[]{:S(2)}) %collective-permute-start.19) | collective-permute-done | bytes 524320 | tf_op jit(solution)/shard_map/ppermute | solution.py:406
  259.4 17.2 %collective-permute-done.17.refs_1_ = f32[1024,128]{1,0:T(8,128)S(1)} collective-permute-done((f32[1024,128]{1,0:T(8,128)S(1)}, f32[1024,128]{1,0:T(8,128)S(1)}, u32[]{:S(2)}, u32[]{:S(2)}) %collective-permute-start.17) | collective-permute-done | bytes 524320 | tf_op jit(solution)/shard_map/ppermute | solution.py:406
  276.6 1.4 finish.13
  (81 shorter events, 32.2 us)
Async XLA Ops:
  1.6 31.6 %collective-permute-start.10 = (f32[256,128]{1,0:T(8,128)S(1)}, f32[256,128]{1,0:T(8,128)}, u32[]{:S(2)}, u32[]{:S(2)}) collective-permute-start(f32[256,128]{1,0:T(8,128)S(1)} %get-tuple-element.95), channel_id=1, source_target_pairs={{0,3},{1,0},{2,1},{3,2},{4,7},{5,4},{6,5},{7,6},{8,11},{9,8},{10,9... | collective-permute-start | bytes 393224 | tf_op jit(solution)/shard_map/ppermute | solution.py:362
  2.1 31.8 %collective-permute-start.9 = (f32[256,128]{1,0:T(8,128)S(1)}, f32[256,128]{1,0:T(8,128)}, u32[]{:S(2)}, u32[]{:S(2)}) collective-permute-start(f32[256,128]{1,0:T(8,128)S(1)} %get-tuple-element.95), channel_id=1, source_target_pairs={{0,2},{1,3},{2,0},{3,1},{4,6},{5,7},{6,4},{7,5},{8,10},{9,11},{10,... | collective-permute-start | bytes 393224 | tf_op jit(solution)/shard_map/ppermute | solution.py:362
  3.6 7.0 %collective-permute-start = (f32[272,128]{1,0:T(8,128)S(1)}, f32[272,128]{1,0:T(8,128)S(1)}, u32[]{:S(2)}, u32[]{:S(2)}) collective-permute-start(f32[272,128]{1,0:T(8,128)S(1)} %get-tuple-element.48), channel_id=1, source_target_pairs={{0,28},{4,24},{8,20},{12,16},{16,12},{20,8},{24,4},{28,0},{1,29},{... | collective-permute-start | bytes 417800 | tf_op jit(solution)/shard_map/ppermute | solution.py:372
  5.3 8.3 %collective-permute-start.1 = (f32[272,128]{1,0:T(8,128)S(1)}, f32[272,128]{1,0:T(8,128)S(1)}, u32[]{:S(2)}, u32[]{:S(2)}) collective-permute-start(f32[272,128]{1,0:T(8,128)S(1)} %get-tuple-element.49), channel_id=1, source_target_pairs={{0,24},{4,28},{8,16},{12,20},{16,8},{20,12},{24,0},{28,4},{1,25},{... | collective-permute-start | bytes 417800 | tf_op jit(solution)/shard_map/ppermute | solution.py:372
  9.1 7.3 %collective-permute-start.2 = (f32[272,128]{1,0:T(8,128)S(1)}, f32[272,128]{1,0:T(8,128)S(1)}, u32[]{:S(2)}, u32[]{:S(2)}) collective-permute-start(f32[272,128]{1,0:T(8,128)S(1)} %get-tuple-element.50), channel_id=1, source_target_pairs={{0,20},{4,16},{8,28},{12,24},{16,4},{20,0},{24,12},{28,8},{1,21},{... | collective-permute-start | bytes 417800 | tf_op jit(solution)/shard_map/ppermute | solution.py:372
  10.6 8.9 %collective-permute-start.3 = (f32[272,128]{1,0:T(8,128)S(1)}, f32[272,128]{1,0:T(8,128)S(1)}, u32[]{:S(2)}, u32[]{:S(2)}) collective-permute-start(f32[272,128]{1,0:T(8,128)S(1)} %get-tuple-element.51), channel_id=1, source_target_pairs={{0,16},{4,20},{8,24},{12,28},{16,0},{20,4},{24,8},{28,12},{1,17},{... | collective-permute-start | bytes 417800 | tf_op jit(solution)/shard_map/ppermute | solution.py:372
  13.6 6.0 %collective-permute-start.4 = (f32[272,128]{1,0:T(8,128)S(1)}, f32[272,128]{1,0:T(8,128)S(1)}, u32[]{:S(2)}, u32[]{:S(2)}) collective-permute-start(f32[272,128]{1,0:T(8,128)S(1)} %get-tuple-element.52), channel_id=1, source_target_pairs={{0,12},{4,8},{8,4},{12,0},{16,28},{20,24},{24,20},{28,16},{1,13},{... | collective-permute-start | bytes 417800 | tf_op jit(solution)/shard_map/ppermute | solution.py:372
  16.5 5.9 %collective-permute-start.5 = (f32[272,128]{1,0:T(8,128)S(1)}, f32[272,128]{1,0:T(8,128)S(1)}, u32[]{:S(2)}, u32[]{:S(2)}) collective-permute-start(f32[272,128]{1,0:T(8,128)S(1)} %get-tuple-element.53), channel_id=1, source_target_pairs={{0,8},{4,12},{8,0},{12,4},{16,24},{20,28},{24,16},{28,20},{1,9},{5... | collective-permute-start | bytes 417800 | tf_op jit(solution)/shard_map/ppermute | solution.py:372
  19.5 2.9 %collective-permute-start.6 = (f32[272,128]{1,0:T(8,128)S(1)}, f32[272,128]{1,0:T(8,128)S(1)}, u32[]{:S(2)}, u32[]{:S(2)}) collective-permute-start(f32[272,128]{1,0:T(8,128)S(1)} %get-tuple-element.54), channel_id=1, source_target_pairs={{0,4},{4,0},{8,12},{12,8},{16,20},{20,16},{24,28},{28,24},{1,5},{5... | collective-permute-start | bytes 417800 | tf_op jit(solution)/shard_map/ppermute | solution.py:372
  29.9 18.0 %collective-permute-start.12 = (f32[1024,128]{1,0:T(8,128)}, f32[1024,128]{1,0:T(8,128)S(1)}, u32[]{:S(2)}, u32[]{:S(2)}) collective-permute-start(f32[1024,128]{1,0:T(8,128)} %get-tuple-element.63.right_ref.own_ref), channel_id=1, source_target_pairs={{0,1},{4,5},{8,9},{12,13},{16,17},{20,21},{24,25},{28,29}} | collective-permute-start | bytes 1572872 | tf_op jit(solution)/shard_map/ppermute | solution.py:395
  30.8 74.5 %collective-permute-start.30 = (f32[2048,128]{1,0:T(8,128)}, f32[2048,128]{1,0:T(8,128)}, u32[]{:S(2)}, u32[]{:S(2)}) collective-permute-start(f32[2048,128]{1,0:T(8,128)} %get-tuple-element.88.own_ref), channel_id=1, source_target_pairs={{1,2},{5,6},{9,10},{13,14},{17,18},{21,22},{25,26},{29,30}} | collective-permute-start | bytes 3145736 | tf_op jit(solution)/shard_map/ppermute | solution.py:392
  32.4 17.0 %collective-permute-start.13 = (f32[1024,128]{1,0:T(8,128)}, f32[1024,128]{1,0:T(8,128)S(1)}, u32[]{:S(2)}, u32[]{:S(2)}) collective-permute-start(f32[1024,128]{1,0:T(8,128)} %get-tuple-element.66.right_ref.own_ref), channel_id=1, source_target_pairs={{0,1},{4,5},{8,9},{12,13},{16,17},{20,21},{24,25},{28,29}} | collective-permute-start | bytes 1572872 | tf_op jit(solution)/shard_map/ppermute | solution.py:395
  33.1 17.9 %collective-permute-start.14 = (f32[1024,128]{1,0:T(8,128)}, f32[1024,128]{1,0:T(8,128)S(1)}, u32[]{:S(2)}, u32[]{:S(2)}) collective-permute-start(f32[1024,128]{1,0:T(8,128)} %get-tuple-element.69.right_ref.own_ref), channel_id=1, source_target_pairs={{0,1},{4,5},{8,9},{12,13},{16,17},{20,21},{24,25},{28,29}} | collective-permute-start | bytes 1572872 | tf_op jit(solution)/shard_map/ppermute | solution.py:395
  33.8 12.7 %collective-permute-start.8 = (f32[256,128]{1,0:T(8,128)S(1)}, f32[256,128]{1,0:T(8,128)}, u32[]{:S(2)}, u32[]{:S(2)}) collective-permute-start(f32[256,128]{1,0:T(8,128)S(1)} %get-tuple-element.95), channel_id=1, source_target_pairs={{0,1},{1,2},{2,3},{3,0},{4,5},{5,6},{6,7},{7,4},{8,9},{9,10},{10,1... | collective-permute-start | bytes 393224 | tf_op jit(solution)/shard_map/ppermute | solution.py:362
  46.5 0.7 collective-permute-start.11
  47.2 49.7 %collective-permute-start.15 = (f32[1024,128]{1,0:T(8,128)}, f32[1024,128]{1,0:T(8,128)S(1)}, u32[]{:S(2)}, u32[]{:S(2)}) collective-permute-start(f32[1024,128]{1,0:T(8,128)} %get-tuple-element.72.right_ref.own_ref), channel_id=1, source_target_pairs={{0,1},{4,5},{8,9},{12,13},{16,17},{20,21},{24,25},{28,29}} | collective-permute-start | bytes 1572872 | tf_op jit(solution)/shard_map/ppermute | solution.py:395
  47.9 53.1 %collective-permute-start.7 = (f32[1024,128]{1,0:T(8,128)}, f32[1024,128]{1,0:T(8,128)}, u32[]{:S(2)}, u32[]{:S(2)}) collective-permute-start(f32[1024,128]{1,0:T(8,128)} %get-tuple-element.56.right_ref.own_ref), channel_id=1, source_target_pairs={{0,1},{4,5},{8,9},{12,13},{16,17},{20,21},{24,25},{28,29}} | collective-permute-start | bytes 1572872 | tf_op jit(solution)/shard_map/ppermute | solution.py:395
  49.4 56.0 %collective-permute-start.29 = (f32[2048,128]{1,0:T(8,128)}, f32[2048,128]{1,0:T(8,128)}, u32[]{:S(2)}, u32[]{:S(2)}) collective-permute-start(f32[2048,128]{1,0:T(8,128)} %get-tuple-element.88.own_ref), channel_id=1, source_target_pairs={{0,1},{4,5},{8,9},{12,13},{16,17},{20,21},{24,25},{28,29}} | collective-permute-start | bytes 3145736 | tf_op jit(solution)/shard_map/ppermute | solution.py:396
  51.0 54.4 %collective-permute-start.28 = (f32[2048,128]{1,0:T(8,128)}, f32[2048,128]{1,0:T(8,128)}, u32[]{:S(2)}, u32[]{:S(2)}) collective-permute-start(f32[2048,128]{1,0:T(8,128)} %get-tuple-element.88.own_ref), channel_id=1, source_target_pairs={{0,2},{4,6},{8,10},{12,14},{16,18},{20,22},{24,26},{28,30}} | collective-permute-start | bytes 3145736 | tf_op jit(solution)/shard_map/ppermute | solution.py:391
  96.9 83.7 %collective-permute-start.24 = (f32[1024,128]{1,0:T(8,128)S(1)}, f32[1024,128]{1,0:T(8,128)S(1)}, u32[]{:S(2)}, u32[]{:S(2)}) collective-permute-start(f32[1024,128]{1,0:T(8,128)S(1)} %get-tuple-element.84), channel_id=1, source_target_pairs={{1,2},{5,6},{9,10},{13,14},{17,18},{21,22},{25,26},{29,30}} | collective-permute-start | bytes 1572872 | tf_op jit(solution)/shard_map/ppermute | solution.py:406
  113.8 101.3 %collective-permute-start.31 = (f32[2048,128]{1,0:T(8,128)S(1)}, f32[2048,128]{1,0:T(8,128)S(1)}, u32[]{:S(2)}, u32[]{:S(2)}) collective-permute-start(f32[2048,128]{1,0:T(8,128)S(1)} %get-tuple-element.91), channel_id=1, source_target_pairs={{2,3},{6,7},{10,11},{14,15},{18,19},{22,23},{26,27},{30,31}} | collective-permute-start | bytes 3145736 | tf_op jit(solution)/shard_map/ppermute | solution.py:415
  115.1 3.3 %collective-permute-start.26 = (f32[512,128]{1,0:T(8,128)S(1)}, f32[512,128]{1,0:T(8,128)S(1)}, u32[]{:S(2)}, u32[]{:S(2)}) collective-permute-start(f32[512,128]{1,0:T(8,128)S(1)} %get-tuple-element.86), channel_id=1, source_target_pairs={{1,2},{5,6},{9,10},{13,14},{17,18},{21,22},{25,26},{29,30}} | collective-permute-start | bytes 786440 | tf_op jit(solution)/shard_map/ppermute | solution.py:406
  115.7 63.6 %collective-permute-start.27 = (f32[512,128]{1,0:T(8,128)S(1)}, f32[512,128]{1,0:T(8,128)S(1)}, u32[]{:S(2)}, u32[]{:S(2)}) collective-permute-start(f32[512,128]{1,0:T(8,128)S(1)} %get-tuple-element.87), channel_id=1, source_target_pairs={{1,3},{5,7},{9,11},{13,15},{17,19},{21,23},{25,27},{29,31}} | collective-permute-start | bytes 786440 | tf_op jit(solution)/shard_map/ppermute | solution.py:406
  117.0 73.5 %collective-permute-start.25 = (f32[1024,128]{1,0:T(8,128)S(1)}, f32[1024,128]{1,0:T(8,128)S(1)}, u32[]{:S(2)}, u32[]{:S(2)}) collective-permute-start(f32[1024,128]{1,0:T(8,128)S(1)} %get-tuple-element.85), channel_id=1, source_target_pairs={{1,3},{5,7},{9,11},{13,15},{17,19},{21,23},{25,27},{29,31}} | collective-permute-start | bytes 1572872 | tf_op jit(solution)/shard_map/ppermute | solution.py:406
  118.3 73.5 %collective-permute-start.22 = (f32[1024,128]{1,0:T(8,128)S(1)}, f32[1024,128]{1,0:T(8,128)S(1)}, u32[]{:S(2)}, u32[]{:S(2)}) collective-permute-start(f32[1024,128]{1,0:T(8,128)S(1)} %get-tuple-element.82), channel_id=1, source_target_pairs={{1,2},{5,6},{9,10},{13,14},{17,18},{21,22},{25,26},{29,30}} | collective-permute-start | bytes 1572872 | tf_op jit(solution)/shard_map/ppermute | solution.py:406
  179.3 33.7 %collective-permute-start.23 = (f32[1024,128]{1,0:T(8,128)S(1)}, f32[1024,128]{1,0:T(8,128)S(1)}, u32[]{:S(2)}, u32[]{:S(2)}) collective-permute-start(f32[1024,128]{1,0:T(8,128)S(1)} %get-tuple-element.83), channel_id=1, source_target_pairs={{1,3},{5,7},{9,11},{13,15},{17,19},{21,23},{25,27},{29,31}} | collective-permute-start | bytes 1572872 | tf_op jit(solution)/shard_map/ppermute | solution.py:406
  180.6 33.7 %collective-permute-start.20 = (f32[1024,128]{1,0:T(8,128)S(1)}, f32[1024,128]{1,0:T(8,128)S(1)}, u32[]{:S(2)}, u32[]{:S(2)}) collective-permute-start(f32[1024,128]{1,0:T(8,128)S(1)} %get-tuple-element.80), channel_id=1, source_target_pairs={{1,2},{5,6},{9,10},{13,14},{17,18},{21,22},{25,26},{29,30}} | collective-permute-start | bytes 1572872 | tf_op jit(solution)/shard_map/ppermute | solution.py:406
  190.6 45.0 %collective-permute-start.21 = (f32[1024,128]{1,0:T(8,128)S(1)}, f32[1024,128]{1,0:T(8,128)S(1)}, u32[]{:S(2)}, u32[]{:S(2)}) collective-permute-start(f32[1024,128]{1,0:T(8,128)S(1)} %get-tuple-element.81), channel_id=1, source_target_pairs={{1,3},{5,7},{9,11},{13,15},{17,19},{21,23},{25,27},{29,31}} | collective-permute-start | bytes 1572872 | tf_op jit(solution)/shard_map/ppermute | solution.py:406
  191.9 45.1 %collective-permute-start.18 = (f32[1024,128]{1,0:T(8,128)S(1)}, f32[1024,128]{1,0:T(8,128)S(1)}, u32[]{:S(2)}, u32[]{:S(2)}) collective-permute-start(f32[1024,128]{1,0:T(8,128)S(1)} %get-tuple-element.78), channel_id=1, source_target_pairs={{1,2},{5,6},{9,10},{13,14},{17,18},{21,22},{25,26},{29,30}} | collective-permute-start | bytes 1572872 | tf_op jit(solution)/shard_map/ppermute | solution.py:406
  213.1 44.9 %collective-permute-start.19 = (f32[1024,128]{1,0:T(8,128)S(1)}, f32[1024,128]{1,0:T(8,128)S(1)}, u32[]{:S(2)}, u32[]{:S(2)}) collective-permute-start(f32[1024,128]{1,0:T(8,128)S(1)} %get-tuple-element.79), channel_id=1, source_target_pairs={{1,3},{5,7},{9,11},{13,15},{17,19},{21,23},{25,27},{29,31}} | collective-permute-start | bytes 1572872 | tf_op jit(solution)/shard_map/ppermute | solution.py:406
  214.4 45.0 %collective-permute-start.16 = (f32[1024,128]{1,0:T(8,128)S(1)}, f32[1024,128]{1,0:T(8,128)S(1)}, u32[]{:S(2)}, u32[]{:S(2)}) collective-permute-start(f32[1024,128]{1,0:T(8,128)S(1)} %get-tuple-element.76), channel_id=1, source_target_pairs={{1,2},{5,6},{9,10},{13,14},{17,18},{21,22},{25,26},{29,30}} | collective-permute-start | bytes 1572872 | tf_op jit(solution)/shard_map/ppermute | solution.py:406
  215.1 61.5 %collective-permute-start.17 = (f32[1024,128]{1,0:T(8,128)S(1)}, f32[1024,128]{1,0:T(8,128)S(1)}, u32[]{:S(2)}, u32[]{:S(2)}) collective-permute-start(f32[1024,128]{1,0:T(8,128)S(1)} %get-tuple-element.77), channel_id=1, source_target_pairs={{1,3},{5,7},{9,11},{13,15},{17,19},{21,23},{25,27},{29,31}} | collective-permute-start | bytes 1572872 | tf_op jit(solution)/shard_map/ppermute | solution.py:406
  (8 other events, 264.5 us)

commit v2 on v1

--- a/solution.py
+++ b/solution.py
@@ -16,7 +16,8 @@
 HBM = pl.BlockSpec(memory_space=pltpu.HBM)
 RAW_ROWS = 2048
 FIRST_ROWS = 512
-CHUNKS = 6
+LAST_ROWS = 256
+CHUNKS = 7
 
 
 def grant(mib):
@@ -92,23 +93,30 @@
 
 
 def assemble_kernel(rows_ref, front_ref, *refs, window, sources):
-    block_refs, out_refs, (sums_ref, sem) = refs[:sources], refs[sources:-2], refs[-2:]
+    block_refs, out_refs = refs[:sources], refs[sources:-4]
+    rows_held, delta_ref, load_sem, sem = refs[-4:]
     width = rows_ref.shape[1]
     slots = rows_ref.shape[0] // sources
-    batch = 16
-    load = pltpu.make_async_copy(front_ref.at[pl.ds(window, sums_ref.shape[0])], sums_ref, sem.at[0])
+    batch, tile = 16, 256
+    total = delta_ref.shape[0]
+    load = pltpu.make_async_copy(front_ref.at[pl.ds(window, total)], rows_held, load_sem)
     load.start()
-    load.wait()
+
+    def clear(i, carry):
+        delta_ref[pl.ds(pl.multiple_of(i * tile, tile), tile), :] = jnp.zeros((tile, width), jnp.float32)
+        return carry
+
+    lax.fori_loop(0, total // tile, clear, 0)
 
     def add_slot(block_ref, block, base):
         for first in range(0, width, batch):
             targets = [rows_ref[block, first + i] - window for i in range(batch)]
             sums = [
-                sums_ref[pl.ds(targets[i], 1), :] + block_ref[pl.ds(base + first + i, 1), :]
+                delta_ref[pl.ds(targets[i], 1), :] + block_ref[pl.ds(base + first + i, 1), :]
                 for i in range(batch)
             ]
             for i in range(batch):
-                sums_ref[pl.ds(targets[i], 1), :] = sums[i]
+                delta_ref[pl.ds(targets[i], 1), :] = sums[i]
 
     for source, block_ref in enumerate(block_refs):
 
@@ -117,13 +125,20 @@
             return carry
 
         lax.fori_loop(0, slots, add, 0)
+    load.wait()
+
+    def join(i, carry):
+        rows = pl.ds(pl.multiple_of(i * tile, tile), tile)
+        delta_ref[rows, :] = rows_held[rows, :] + delta_ref[rows, :]
+        return carry
+
     copies, first = [], 0
     for i, ref in enumerate(out_refs):
-        rows = pl.ds(first, ref.shape[0])
-        copies.append(pltpu.make_async_copy(sums_ref.at[rows], ref, sem.at[i]))
-        first += ref.shape[0]
-    for copy in copies:
-        copy.start()
+        last = first + ref.shape[0]
+        lax.fori_loop(first // tile, last // tile, join, 0)
+        copies.append(pltpu.make_async_copy(delta_ref.at[pl.ds(first, ref.shape[0])], ref, sem.at[i]))
+        copies[-1].start()
+        first = last
     for copy in copies:
         copy.wait()
 
@@ -138,9 +153,11 @@
         out_shape=[pltpu.HBM((size, width), jnp.float32) for size in sizes],
         scratch_shapes=[
             pltpu.VMEM((front.shape[0] - window, width), jnp.float32),
+            pltpu.VMEM((front.shape[0] - window, width), jnp.float32),
+            pltpu.SemaphoreType.DMA,
             pltpu.SemaphoreType.DMA((len(sizes),)),
         ],
-        compiler_params=grant(6),
+        compiler_params=grant(10),
         name="assemble",
     )(rows, in_hbm(front), *held)
 
@@ -335,12 +352,13 @@
 
 
 def cut_rows(first, last):
-    rest = last - first - RAW_ROWS - FIRST_ROWS
-    size = -(-rest // ((CHUNKS - 1) * 256)) * 256
+    rest = last - first - RAW_ROWS - FIRST_ROWS - LAST_ROWS
+    size = -(-rest // ((CHUNKS - 2) * 256)) * 256
     sizes = [RAW_ROWS, FIRST_ROWS]
     while rest > 0:
         sizes.append(min(size, rest))
         rest -= sizes[-1]
+    sizes.append(LAST_ROWS)
     return [first + sum(sizes[:i]) for i in range(len(sizes))], sizes
 
 

time: 279 us -> 280 us (level)
  the two profiles are of different devices: /device:TPU:24 before, /device:TPU:26 now
where the time goes in v2:
time: 280 us; the launch traced here: 279 us
  waiting for transfers between devices  160 us (57%)
  Pallas kernels  76.1 us (27%)
  starting transfers between devices  34.5 us (12%)
  local copies, waits for them, and re-layouts  4.55 us (2%)
    ppermute x14, waiting for transfers between devices, extend_and_factor(): moved.append(lax.ppermute(u, 'blk', [(1, block)]))  146 us
    pallas_call x1, Pallas kernels, factor(): pl.pallas_call(factor_kernel, grid=(1,), in_specs=[SMEM, tops_spec, windo...  29.8 us
    pallas_call x8, Pallas kernels, multiply(): pl.pallas_call(multiply_kernel, grid=(rows // tile,), in_specs=[spec, spe...  25.2 us
    ppermute x7, waiting for transfers between devices, extend_and_factor(): block = lax.ppermute(block, 'group', pairs)  14.2 us
    ppermute x14, starting transfers between devices, extend_and_factor(): moved.append(lax.ppermute(u, 'blk', [(1, block)]))  14 us
    pallas_call x8, Pallas kernels, finish(): pl.pallas_call(finish_kernel, grid=(rows // tile,), in_specs=[SMEM] + [sp...  11.1 us
    pallas_call x1, Pallas kernels, assemble(): pl.pallas_call(functools.partial(assemble_kernel, window=window, sources=...  5.79 us
  transfers between devices with their start and end apart: 35, of which 11 were waited for; matrix products, arithmetic and copies ran while one was open for 1% of the time, Pallas kernels for 27%

profile of v2, /device:TPU:26, one launch (start us, length us, event | category | flops | bytes accessed | tf_op | source)
XLA Modules:
  0.0 279.5 jit_solution(17399291416704722890)
XLA Ops:
  0.6 1.6 fusion
  3.0 3.0 %collective-permute-start.8 = (f32[256,128]{1,0:T(8,128)S(1)}, f32[256,128]{1,0:T(8,128)}, u32[]{:S(2)}, u32[]{:S(2)}) collective-permute-start(f32[256,128]{1,0:T(8,128)S(1)} %get-tuple-element.105), channel_id=1, source_target_pairs={{0,1},{1,2},{2,3},{3,0},{4,5},{5,6},{6,7},{7,4},{8,9},{9,10},{10,1... | collective-permute-start | bytes 393224 | tf_op jit(solution)/shard_map/ppermute | solution.py:380
  6.0 1.5 pack.2
  8.0 1.4 collective-permute-start.1
  9.4 2.6 pack.3
  12.0 2.5 collective-permute-done.refs_0_
  14.7 1.6 collective-permute-done.1.refs_1_
  16.4 1.5 collective-permute-start.3
  17.9 2.5 collective-permute-done.2.refs_2_
  20.8 2.6 collective-permute-done.3.refs_3_
  24.0 2.1 collective-permute-done.4.refs_4_
  26.5 2.9 %collective-permute-done.5.refs_5_ = f32[272,128]{1,0:T(8,128)S(1)} collective-permute-done((f32[272,128]{1,0:T(8,128)S(1)}, f32[272,128]{1,0:T(8,128)S(1)}, u32[]{:S(2)}, u32[]{:S(2)}) %collective-permute-start.5) | collective-permute-done | bytes 139296 | tf_op jit(solution)/shard_map/ppermute | solution.py:390
  29.4 5.8 %assemble.1 = (f32[2048,128]{1,0:T(8,128)}, f32[512,128]{1,0:T(8,128)}, f32[1024,128]{1,0:T(8,128)}, f32[1024,128]{1,0:T(8,128)}, f32[1024,128]{1,0:T(8,128)}, /...) custom-call(s32[16,128]{1,0:T(8,128)S(1)} %convert_element_type.3.rows_ref, f32[8192,128]{1,0:T(8,128)} %bitcast.13, ...), custom_call_target="tpu_custom_call" | custom-call | tf_op jit(solution)/shard_map/assemble/pallas_call | solution.py:149
  35.2 1.8 collective-permute-start.33
  41.2 1.6 collective-permute-start.32
  42.9 1.7 collective-permute-start.31
  47.7 2.2 copy-done
  49.9 29.8 %factor.1 = (f32[3,256,128]{2,1,0:T(8,128)S(1)}, f32[8192,128]{1,0:T(8,128)}, f32[1,256]{1,0:T(1,128)}) custom-call(s32[1]{0:T(128)} %bitcast.index_ref, f32[4,256,128]{2,1,0:T(8,128)S(1)} %pad_maximum_fusion.tops_ref, f32[8192,128]{1,0:T(8,128)S(1)} %bitcast.14), custom_call_target="tpu_custom_call" | custom-call | tf_op jit(solution)/shard_map/factor/pallas_call | solution.py:282
  79.7 1.6 multiply.8
  81.3 3.2 %multiply.9 = (f32[1024,128]{1,0:T(8,128)S(1)}, f32[1024,128]{1,0:T(8,128)S(1)}, f32[1024,128]{1,0:T(8,128)S(1)}) custom-call(f32[1024,128]{1,0:T(8,128)S(1)} %collective-permute-done.12.left_ref, f32[1024,128]{1,0:T(8,128)S(1)} %copy-done.5, f32[3,256,128]{2,1,0:T(8,128)S(1)} %get-tuple-element.99.weights_ref), custom_call_target="tpu_custom_call" | custom-call | tf_op jit(solution)/shard_map/multiply/pallas_call | solution.py:311
  84.5 3.2 %multiply.10 = (f32[1024,128]{1,0:T(8,128)S(1)}, f32[1024,128]{1,0:T(8,128)S(1)}, f32[1024,128]{1,0:T(8,128)S(1)}) custom-call(f32[1024,128]{1,0:T(8,128)S(1)} %collective-permute-done.13.left_ref, f32[1024,128]{1,0:T(8,128)S(1)} %copy-done.4, f32[3,256,128]{2,1,0:T(8,128)S(1)} %get-tuple-element.99.weights_ref), custom_call_target="tpu_custom_call" | custom-call | tf_op jit(solution)/shard_map/multiply/pallas_call | solution.py:311
  87.7 3.2 %multiply.11 = (f32[1024,128]{1,0:T(8,128)S(1)}, f32[1024,128]{1,0:T(8,128)S(1)}, f32[1024,128]{1,0:T(8,128)S(1)}) custom-call(f32[1024,128]{1,0:T(8,128)S(1)} %collective-permute-done.14.left_ref, f32[1024,128]{1,0:T(8,128)S(1)} %copy-done.3, f32[3,256,128]{2,1,0:T(8,128)S(1)} %get-tuple-element.99.weights_ref), custom_call_target="tpu_custom_call" | custom-call | tf_op jit(solution)/shard_map/multiply/pallas_call | solution.py:311
  90.9 3.2 %multiply.12 = (f32[1024,128]{1,0:T(8,128)S(1)}, f32[1024,128]{1,0:T(8,128)S(1)}, f32[1024,128]{1,0:T(8,128)S(1)}) custom-call(f32[1024,128]{1,0:T(8,128)S(1)} %collective-permute-done.15.left_ref, f32[1024,128]{1,0:T(8,128)S(1)} %copy-done.2, f32[3,256,128]{2,1,0:T(8,128)S(1)} %get-tuple-element.99.weights_ref), custom_call_target="tpu_custom_call" | custom-call | tf_op jit(solution)/shard_map/multiply/pallas_call | solution.py:311
  94.7 2.4 multiply.13
  98.0 1.7 multiply.14
  103.2 7.0 %multiply.15 = (f32[2048,128]{1,0:T(8,128)S(1)}, f32[2048,128]{1,0:T(8,128)}, f32[2048,128]{1,0:T(8,128)S(1)}) custom-call(f32[2048,128]{1,0:T(8,128)S(1)} %broadcast_select_fusion.2.left_ref, f32[2048,128]{1,0:T(8,128)S(1)} %broadcast_select_fusion.1.right_ref, f32[3,256,128]{2,1,0:T(8,128)S(1)} %get-tuple-element.99.weights_ref), custom_call_target="tpu_custom_call" | custom-call | tf_op jit(solution)/shard_map/multiply/pallas_call | solution.py:311
  112.8 84.5 %collective-permute-done.30.refs_1_ = f32[512,128]{1,0:T(8,128)S(1)} collective-permute-done((f32[512,128]{1,0:T(8,128)S(1)}, f32[512,128]{1,0:T(8,128)S(1)}, u32[]{:S(2)}, u32[]{:S(2)}) %collective-permute-start.30) | collective-permute-done | bytes 262176 | tf_op jit(solution)/shard_map/ppermute | solution.py:424
  201.3 13.6 %collective-permute-done.26.refs_1_ = f32[1024,128]{1,0:T(8,128)S(1)} collective-permute-done((f32[1024,128]{1,0:T(8,128)S(1)}, f32[1024,128]{1,0:T(8,128)S(1)}, u32[]{:S(2)}, u32[]{:S(2)}) %collective-permute-start.26) | collective-permute-done | bytes 524320 | tf_op jit(solution)/shard_map/ppermute | solution.py:424
  216.8 20.5 %collective-permute-done.24.refs_1_ = f32[1024,128]{1,0:T(8,128)S(1)} collective-permute-done((f32[1024,128]{1,0:T(8,128)S(1)}, f32[1024,128]{1,0:T(8,128)S(1)}, u32[]{:S(2)}, u32[]{:S(2)}) %collective-permute-start.24) | collective-permute-done | bytes 524320 | tf_op jit(solution)/shard_map/ppermute | solution.py:424
  240.7 2.8 finish.8.refs_2_
  248.4 11.4 %collective-permute-done.22.refs_1_ = f32[1024,128]{1,0:T(8,128)S(1)} collective-permute-done((f32[1024,128]{1,0:T(8,128)S(1)}, f32[1024,128]{1,0:T(8,128)S(1)}, u32[]{:S(2)}, u32[]{:S(2)}) %collective-permute-start.22) | collective-permute-done | bytes 524320 | tf_op jit(solution)/shard_map/ppermute | solution.py:424
  261.2 16.2 %collective-permute-done.20.refs_1_ = f32[768,128]{1,0:T(8,128)S(1)} collective-permute-done((f32[768,128]{1,0:T(8,128)S(1)}, f32[768,128]{1,0:T(8,128)S(1)}, u32[]{:S(2)}, u32[]{:S(2)}) %collective-permute-start.20) | collective-permute-done | bytes 393248 | tf_op jit(solution)/shard_map/ppermute | solution.py:424
  (95 shorter events, 35.3 us)
Async XLA Ops:
  2.2 35.5 %collective-permute-start.10 = (f32[256,128]{1,0:T(8,128)S(1)}, f32[256,128]{1,0:T(8,128)}, u32[]{:S(2)}, u32[]{:S(2)}) collective-permute-start(f32[256,128]{1,0:T(8,128)S(1)} %get-tuple-element.105), channel_id=1, source_target_pairs={{0,3},{1,0},{2,1},{3,2},{4,7},{5,4},{6,5},{7,6},{8,11},{9,8},{10,9... | collective-permute-start | bytes 393224 | tf_op jit(solution)/shard_map/ppermute | solution.py:380
  2.7 35.8 %collective-permute-start.9 = (f32[256,128]{1,0:T(8,128)S(1)}, f32[256,128]{1,0:T(8,128)}, u32[]{:S(2)}, u32[]{:S(2)}) collective-permute-start(f32[256,128]{1,0:T(8,128)S(1)} %get-tuple-element.105), channel_id=1, source_target_pairs={{0,2},{1,3},{2,0},{3,1},{4,6},{5,7},{6,4},{7,5},{8,10},{9,11},{10,... | collective-permute-start | bytes 393224 | tf_op jit(solution)/shard_map/ppermute | solution.py:380
  3.0 36.1 %collective-permute-start.8 = (f32[256,128]{1,0:T(8,128)S(1)}, f32[256,128]{1,0:T(8,128)}, u32[]{:S(2)}, u32[]{:S(2)}) collective-permute-start(f32[256,128]{1,0:T(8,128)S(1)} %get-tuple-element.105), channel_id=1, source_target_pairs={{0,1},{1,2},{2,3},{3,0},{4,5},{5,6},{6,7},{7,4},{8,9},{9,10},{10,1... | collective-permute-start | bytes 393224 | tf_op jit(solution)/shard_map/ppermute | solution.py:380
  7.6 6.9 %collective-permute-start = (f32[272,128]{1,0:T(8,128)S(1)}, f32[272,128]{1,0:T(8,128)S(1)}, u32[]{:S(2)}, u32[]{:S(2)}) collective-permute-start(f32[272,128]{1,0:T(8,128)S(1)} %get-tuple-element.53), channel_id=1, source_target_pairs={{0,28},{4,24},{8,20},{12,16},{16,12},{20,8},{24,4},{28,0},{1,29},{... | collective-permute-start | bytes 417800 | tf_op jit(solution)/shard_map/ppermute | solution.py:390
  8.0 8.4 %collective-permute-start.1 = (f32[272,128]{1,0:T(8,128)S(1)}, f32[272,128]{1,0:T(8,128)S(1)}, u32[]{:S(2)}, u32[]{:S(2)}) collective-permute-start(f32[272,128]{1,0:T(8,128)S(1)} %get-tuple-element.54), channel_id=1, source_target_pairs={{0,24},{4,28},{8,16},{12,20},{16,8},{20,12},{24,0},{28,4},{1,25},{... | collective-permute-start | bytes 417800 | tf_op jit(solution)/shard_map/ppermute | solution.py:390
  14.5 5.9 %collective-permute-start.2 = (f32[272,128]{1,0:T(8,128)S(1)}, f32[272,128]{1,0:T(8,128)S(1)}, u32[]{:S(2)}, u32[]{:S(2)}) collective-permute-start(f32[272,128]{1,0:T(8,128)S(1)} %get-tuple-element.55), channel_id=1, source_target_pairs={{0,20},{4,16},{8,28},{12,24},{16,4},{20,0},{24,12},{28,8},{1,21},{... | collective-permute-start | bytes 417800 | tf_op jit(solution)/shard_map/ppermute | solution.py:390
  16.4 7.1 %collective-permute-start.3 = (f32[272,128]{1,0:T(8,128)S(1)}, f32[272,128]{1,0:T(8,128)S(1)}, u32[]{:S(2)}, u32[]{:S(2)}) collective-permute-start(f32[272,128]{1,0:T(8,128)S(1)} %get-tuple-element.56), channel_id=1, source_target_pairs={{0,16},{4,20},{8,24},{12,28},{16,0},{20,4},{24,8},{28,12},{1,17},{... | collective-permute-start | bytes 417800 | tf_op jit(solution)/shard_map/ppermute | solution.py:390
  20.4 5.7 %collective-permute-start.4 = (f32[272,128]{1,0:T(8,128)S(1)}, f32[272,128]{1,0:T(8,128)S(1)}, u32[]{:S(2)}, u32[]{:S(2)}) collective-permute-start(f32[272,128]{1,0:T(8,128)S(1)} %get-tuple-element.57), channel_id=1, source_target_pairs={{0,12},{4,8},{8,4},{12,0},{16,28},{20,24},{24,20},{28,16},{1,13},{... | collective-permute-start | bytes 417800 | tf_op jit(solution)/shard_map/ppermute | solution.py:390
  23.5 5.9 %collective-permute-start.5 = (f32[272,128]{1,0:T(8,128)S(1)}, f32[272,128]{1,0:T(8,128)S(1)}, u32[]{:S(2)}, u32[]{:S(2)}) collective-permute-start(f32[272,128]{1,0:T(8,128)S(1)} %get-tuple-element.58), channel_id=1, source_target_pairs={{0,8},{4,12},{8,0},{12,4},{16,24},{20,28},{24,16},{28,20},{1,9},{5... | collective-permute-start | bytes 417800 | tf_op jit(solution)/shard_map/ppermute | solution.py:390
  35.2 64.5 %collective-permute-start.33 = (f32[2048,128]{1,0:T(8,128)}, f32[2048,128]{1,0:T(8,128)}, u32[]{:S(2)}, u32[]{:S(2)}) collective-permute-start(f32[2048,128]{1,0:T(8,128)} %get-tuple-element.98.own_ref), channel_id=1, source_target_pairs={{1,2},{5,6},{9,10},{13,14},{17,18},{21,22},{25,26},{29,30}} | collective-permute-start | bytes 3145736 | tf_op jit(solution)/shard_map/ppermute | solution.py:410
  37.7 5.2 %collective-permute-start.13 = (f32[1024,128]{1,0:T(8,128)}, f32[1024,128]{1,0:T(8,128)S(1)}, u32[]{:S(2)}, u32[]{:S(2)}) collective-permute-start(f32[1024,128]{1,0:T(8,128)} %get-tuple-element.71.right_ref.own_ref), channel_id=1, source_target_pairs={{0,1},{4,5},{8,9},{12,13},{16,17},{20,21},{24,25},{28,29}} | collective-permute-start | bytes 1572872 | tf_op jit(solution)/shard_map/ppermute | solution.py:413
  38.4 6.1 %collective-permute-start.14 = (f32[1024,128]{1,0:T(8,128)}, f32[1024,128]{1,0:T(8,128)S(1)}, u32[]{:S(2)}, u32[]{:S(2)}) collective-permute-start(f32[1024,128]{1,0:T(8,128)} %get-tuple-element.74.right_ref.own_ref), channel_id=1, source_target_pairs={{0,1},{4,5},{8,9},{12,13},{16,17},{20,21},{24,25},{28,29}} | collective-permute-start | bytes 1572872 | tf_op jit(solution)/shard_map/ppermute | solution.py:413
  40.5 4.7 %collective-permute-start.15 = (f32[1024,128]{1,0:T(8,128)}, f32[1024,128]{1,0:T(8,128)S(1)}, u32[]{:S(2)}, u32[]{:S(2)}) collective-permute-start(f32[1024,128]{1,0:T(8,128)} %get-tuple-element.77.right_ref.own_ref), channel_id=1, source_target_pairs={{0,1},{4,5},{8,9},{12,13},{16,17},{20,21},{24,25},{28,29}} | collective-permute-start | bytes 1572872 | tf_op jit(solution)/shard_map/ppermute | solution.py:413
  41.2 59.9 %collective-permute-start.32 = (f32[2048,128]{1,0:T(8,128)}, f32[2048,128]{1,0:T(8,128)}, u32[]{:S(2)}, u32[]{:S(2)}) collective-permute-start(f32[2048,128]{1,0:T(8,128)} %get-tuple-element.98.own_ref), channel_id=1, source_target_pairs={{0,1},{4,5},{8,9},{12,13},{16,17},{20,21},{24,25},{28,29}} | collective-permute-start | bytes 3145736 | tf_op jit(solution)/shard_map/ppermute | solution.py:414
  42.9 59.0 %collective-permute-start.31 = (f32[2048,128]{1,0:T(8,128)}, f32[2048,128]{1,0:T(8,128)}, u32[]{:S(2)}, u32[]{:S(2)}) collective-permute-start(f32[2048,128]{1,0:T(8,128)} %get-tuple-element.98.own_ref), channel_id=1, source_target_pairs={{0,2},{4,6},{8,10},{12,14},{16,18},{20,22},{24,26},{28,30}} | collective-permute-start | bytes 3145736 | tf_op jit(solution)/shard_map/ppermute | solution.py:409
  44.6 49.5 %collective-permute-start.16 = (f32[768,128]{1,0:T(8,128)}, f32[768,128]{1,0:T(8,128)S(1)}, u32[]{:S(2)}, u32[]{:S(2)}) collective-permute-start(f32[768,128]{1,0:T(8,128)} %get-tuple-element.80.right_ref.own_ref), channel_id=1, source_target_pairs={{0,1},{4,5},{8,9},{12,13},{16,17},{20,21},{24,25},{28,29}} | collective-permute-start | bytes 1179656 | tf_op jit(solution)/shard_map/ppermute | solution.py:413
  45.2 51.9 %collective-permute-start.7 = (f32[256,128]{1,0:T(8,128)}, f32[256,128]{1,0:T(8,128)}, u32[]{:S(2)}, u32[]{:S(2)}) collective-permute-start(f32[256,128]{1,0:T(8,128)} %get-tuple-element.61.right_ref.own_ref), channel_id=1, source_target_pairs={{0,1},{4,5},{8,9},{12,13},{16,17},{20,21},{24,25},{28,29}} | collective-permute-start | bytes 393224 | tf_op jit(solution)/shard_map/ppermute | solution.py:413
  94.0 17.5 %collective-permute-start.29 = (f32[512,128]{1,0:T(8,128)S(1)}, f32[512,128]{1,0:T(8,128)S(1)}, u32[]{:S(2)}, u32[]{:S(2)}) collective-permute-start(f32[512,128]{1,0:T(8,128)S(1)} %get-tuple-element.96), channel_id=1, source_target_pairs={{1,2},{5,6},{9,10},{13,14},{17,18},{21,22},{25,26},{29,30}} | collective-permute-start | bytes 786440 | tf_op jit(solution)/shard_map/ppermute | solution.py:424
  97.1 101.4 %collective-permute-start.27 = (f32[1024,128]{1,0:T(8,128)S(1)}, f32[1024,128]{1,0:T(8,128)S(1)}, u32[]{:S(2)}, u32[]{:S(2)}) collective-permute-start(f32[1024,128]{1,0:T(8,128)S(1)} %get-tuple-element.94), channel_id=1, source_target_pairs={{1,2},{5,6},{9,10},{13,14},{17,18},{21,22},{25,26},{29,30}} | collective-permute-start | bytes 1572872 | tf_op jit(solution)/shard_map/ppermute | solution.py:424
  99.7 99.6 %collective-permute-start.28 = (f32[1024,128]{1,0:T(8,128)S(1)}, f32[1024,128]{1,0:T(8,128)S(1)}, u32[]{:S(2)}, u32[]{:S(2)}) collective-permute-start(f32[1024,128]{1,0:T(8,128)S(1)} %get-tuple-element.95), channel_id=1, source_target_pairs={{1,3},{5,7},{9,11},{13,15},{17,19},{21,23},{25,27},{29,31}} | collective-permute-start | bytes 1572872 | tf_op jit(solution)/shard_map/ppermute | solution.py:424
  101.2 99.4 %collective-permute-start.25 = (f32[1024,128]{1,0:T(8,128)S(1)}, f32[1024,128]{1,0:T(8,128)S(1)}, u32[]{:S(2)}, u32[]{:S(2)}) collective-permute-start(f32[1024,128]{1,0:T(8,128)S(1)} %get-tuple-element.92), channel_id=1, source_target_pairs={{1,2},{5,6},{9,10},{13,14},{17,18},{21,22},{25,26},{29,30}} | collective-permute-start | bytes 1572872 | tf_op jit(solution)/shard_map/ppermute | solution.py:424
  110.2 129.1 %collective-permute-start.34 = (f32[2048,128]{1,0:T(8,128)S(1)}, f32[2048,128]{1,0:T(8,128)S(1)}, u32[]{:S(2)}, u32[]{:S(2)}) collective-permute-start(f32[2048,128]{1,0:T(8,128)S(1)} %get-tuple-element.101), channel_id=1, source_target_pairs={{2,3},{6,7},{10,11},{14,15},{18,19},{22,23},{26,27},{30,31}} | collective-permute-start | bytes 3145736 | tf_op jit(solution)/shard_map/ppermute | solution.py:433
  111.5 85.8 %collective-permute-start.30 = (f32[512,128]{1,0:T(8,128)S(1)}, f32[512,128]{1,0:T(8,128)S(1)}, u32[]{:S(2)}, u32[]{:S(2)}) collective-permute-start(f32[512,128]{1,0:T(8,128)S(1)} %get-tuple-element.97), channel_id=1, source_target_pairs={{1,3},{5,7},{9,11},{13,15},{17,19},{21,23},{25,27},{29,31}} | collective-permute-start | bytes 786440 | tf_op jit(solution)/shard_map/ppermute | solution.py:424
  197.3 17.6 %collective-permute-start.26 = (f32[1024,128]{1,0:T(8,128)S(1)}, f32[1024,128]{1,0:T(8,128)S(1)}, u32[]{:S(2)}, u32[]{:S(2)}) collective-permute-start(f32[1024,128]{1,0:T(8,128)S(1)} %get-tuple-element.93), channel_id=1, source_target_pairs={{1,3},{5,7},{9,11},{13,15},{17,19},{21,23},{25,27},{29,31}} | collective-permute-start | bytes 1572872 | tf_op jit(solution)/shard_map/ppermute | solution.py:424
  198.6 17.6 %collective-permute-start.23 = (f32[1024,128]{1,0:T(8,128)S(1)}, f32[1024,128]{1,0:T(8,128)S(1)}, u32[]{:S(2)}, u32[]{:S(2)}) collective-permute-start(f32[1024,128]{1,0:T(8,128)S(1)} %get-tuple-element.90), channel_id=1, source_target_pairs={{1,2},{5,6},{9,10},{13,14},{17,18},{21,22},{25,26},{29,30}} | collective-permute-start | bytes 1572872 | tf_op jit(solution)/shard_map/ppermute | solution.py:424
  199.3 38.0 %collective-permute-start.24 = (f32[1024,128]{1,0:T(8,128)S(1)}, f32[1024,128]{1,0:T(8,128)S(1)}, u32[]{:S(2)}, u32[]{:S(2)}) collective-permute-start(f32[1024,128]{1,0:T(8,128)S(1)} %get-tuple-element.91), channel_id=1, source_target_pairs={{1,3},{5,7},{9,11},{13,15},{17,19},{21,23},{25,27},{29,31}} | collective-permute-start | bytes 1572872 | tf_op jit(solution)/shard_map/ppermute | solution.py:424
  200.6 38.0 %collective-permute-start.21 = (f32[1024,128]{1,0:T(8,128)S(1)}, f32[1024,128]{1,0:T(8,128)S(1)}, u32[]{:S(2)}, u32[]{:S(2)}) collective-permute-start(f32[1024,128]{1,0:T(8,128)S(1)} %get-tuple-element.88), channel_id=1, source_target_pairs={{1,2},{5,6},{9,10},{13,14},{17,18},{21,22},{25,26},{29,30}} | collective-permute-start | bytes 1572872 | tf_op jit(solution)/shard_map/ppermute | solution.py:424
  214.9 44.9 %collective-permute-start.22 = (f32[1024,128]{1,0:T(8,128)S(1)}, f32[1024,128]{1,0:T(8,128)S(1)}, u32[]{:S(2)}, u32[]{:S(2)}) collective-permute-start(f32[1024,128]{1,0:T(8,128)S(1)} %get-tuple-element.89), channel_id=1, source_target_pairs={{1,3},{5,7},{9,11},{13,15},{17,19},{21,23},{25,27},{29,31}} | collective-permute-start | bytes 1572872 | tf_op jit(solution)/shard_map/ppermute | solution.py:424
  216.2 62.6 %collective-permute-start.17 = (f32[256,128]{1,0:T(8,128)S(1)}, f32[256,128]{1,0:T(8,128)S(1)}, u32[]{:S(2)}, u32[]{:S(2)}) collective-permute-start(f32[256,128]{1,0:T(8,128)S(1)} %get-tuple-element.84), channel_id=1, source_target_pairs={{1,2},{5,6},{9,10},{13,14},{17,18},{21,22},{25,26},{29,30}} | collective-permute-start | bytes 393224 | tf_op jit(solution)/shard_map/ppermute | solution.py:424
  237.3 41.4 %collective-permute-start.18 = (f32[256,128]{1,0:T(8,128)S(1)}, f32[256,128]{1,0:T(8,128)S(1)}, u32[]{:S(2)}, u32[]{:S(2)}) collective-permute-start(f32[256,128]{1,0:T(8,128)S(1)} %get-tuple-element.85), channel_id=1, source_target_pairs={{1,3},{5,7},{9,11},{13,15},{17,19},{21,23},{25,27},{29,31}} | collective-permute-start | bytes 393224 | tf_op jit(solution)/shard_map/ppermute | solution.py:424
  238.6 22.6 %collective-permute-start.19 = (f32[768,128]{1,0:T(8,128)S(1)}, f32[768,128]{1,0:T(8,128)S(1)}, u32[]{:S(2)}, u32[]{:S(2)}) collective-permute-start(f32[768,128]{1,0:T(8,128)S(1)} %get-tuple-element.86), channel_id=1, source_target_pairs={{1,2},{5,6},{9,10},{13,14},{17,18},{21,22},{25,26},{29,30}} | collective-permute-start | bytes 1179656 | tf_op jit(solution)/shard_map/ppermute | solution.py:424
  239.3 38.1 %collective-permute-start.20 = (f32[768,128]{1,0:T(8,128)S(1)}, f32[768,128]{1,0:T(8,128)S(1)}, u32[]{:S(2)}, u32[]{:S(2)}) collective-permute-start(f32[768,128]{1,0:T(8,128)S(1)} %get-tuple-element.87), channel_id=1, source_target_pairs={{1,3},{5,7},{9,11},{13,15},{17,19},{21,23},{25,27},{29,31}} | collective-permute-start | bytes 1179656 | tf_op jit(solution)/shard_map/ppermute | solution.py:424
  (14 other events, 299.5 us)
